TPU v7x, 512 devices: a whole 4x8x8 slice. The times are simulated.
512 devices in a mesh: gz: 8 (over x, z_lo), row: 8 (over z_hi, core), col: 8 (over y).
Axes of the slice: x: 4, y: 8, z: 8 (z_hi: 4, z_lo: 2; z = z_hi * 2 + z_lo), core: 2. Of those that a mesh axis runs over, the one named last changes fastest.
Arguments:
- front: float32 [4096, 4096], P('row', 'col'), may hold values from -0.04 to 1.45
- lower_parts: float32 [8, 4096, 256], P('gz', 'row'), may hold values from -0.1875 to 0.1875
- upper_parts: float32 [8, 256, 4096], P('gz', None, 'col'), may hold values from -0.125 to 0.125
- pattern: int32 [8, 32, 2], P('gz', 'row'), may hold values 0 or 1
- row_perm: int32 [8, 512], P('row'), may hold values from 0 to 511, as said below
Outputs:
- factored: float32 [4096, 4096], P('row', 'col')
Inputs may be any that keep to these rules, and one draw needn't show every extreme that they name: `row_perm`: each of the 8 rows holds every number 0 to 511 once.
All inputs are finite; a program needn't handle non-finite values. No bound on the sum of `pattern` on one device may be relied on, other than what follows from the above.
Results may differ from a plain program's by a relative error of at most 0.0001.
Values sent between devices are 32-bit elements; how exact they have to be, the bound alone decides.
A program may use at most 64 MiB of HBM per device.

v0:
```python
import jax
import jax.numpy as jnp
from jax import lax
from jax.sharding import PartitionSpec as P

BS = 128
NS_STEPS = 3
PANELS = 2


precise = lax.Precision.HIGHEST


def spread(value, axis, root):
    mine = lax.axis_index(axis) == root
    return lax.psum(jnp.where(mine, value, jnp.zeros_like(value)), axis)


def product(first_matrix, second_matrix):
    return jnp.dot(
        first_matrix, second_matrix, precision=precise, preferred_element_type=jnp.float32
    )


def advance_rows(own_rows, pivot_block, full_inverse):
    return 2.0 * own_rows - product(product(own_rows, pivot_block), full_inverse)


def newton_inverse(pivot_block):
    block_width = pivot_block.shape[0]
    full_inverse = 2.0 * jnp.eye(block_width, dtype=jnp.float32) - pivot_block
    for iteration in range(NS_STEPS - 1):
        full_inverse = advance_rows(full_inverse, pivot_block, full_inverse)
    return full_inverse


def on_device(front, lower_parts, upper_parts, pattern, row_perm):
    panel_width = row_perm.shape[1]
    local_rows, local_cols = front.shape
    blocks_down = local_rows // panel_width
    blocks_across = local_cols // panel_width
    inner_cols = lower_parts.shape[2]
    masked = lower_parts[0].reshape(local_rows // BS, BS, inner_cols // BS, BS)
    masked = masked * pattern[0].astype(jnp.float32)[:, None, :, None]
    partial_value = product(masked.reshape(local_rows, inner_cols), upper_parts[0])
    merged = front - lax.psum(partial_value, "gz")
    sources = (jnp.arange(blocks_down, dtype=jnp.int32) * panel_width)[:, None] + row_perm
    factored = jnp.take(merged, sources.reshape(local_rows), axis=0)
    grid_row = lax.axis_index("row")
    grid_col = lax.axis_index("col")
    row_panels = grid_row * blocks_down + jnp.arange(local_rows, dtype=jnp.int32) // panel_width
    col_panels = grid_col * blocks_across + jnp.arange(local_cols, dtype=jnp.int32) // panel_width
    identity = jnp.eye(panel_width, dtype=jnp.float32)
    for panel_index in range(PANELS):
        owner_row = panel_index // blocks_down
        owner_col = panel_index // blocks_across
        row_start = panel_index % blocks_down * panel_width
        col_start = panel_index % blocks_across * panel_width
        panel_row = spread(factored, "row", owner_row)
        in_column = grid_col == owner_col
        pivot_block = jnp.where(in_column, panel_row, identity)
        inverse = newton_inverse(pivot_block)
        column_block = factored
        lower_own = product(column_block, inverse)
        lower_recv = spread(lower_own, "col", owner_col)
        below_rows = row_panels > panel_index
        trailing = below_rows[:, None] & (col_panels > panel_index)[None, :]
        factored = factored - jnp.where(trailing, product(lower_recv, panel_row), 0.0)
        current = factored
        stacked = jnp.tile(inverse, (blocks_down, 1))
        diagonal_rows = row_panels == panel_index
        replaced = jnp.where(
            below_rows[:, None], lower_own, jnp.where(diagonal_rows[:, None], stacked, current)
        )
        factored = factored.at[:, col_start : col_start + panel_width].set(
            jnp.where(in_column, replaced, current)
        )
    return factored


def solution(mesh):
    in_specs = (
        P("row", "col"),
        P("gz", "row", None),
        P("gz", None, "col"),
        P("gz", "row", None),
        P("row", None),
    )
    out_specs = P("row", "col")
    return jax.shard_map(
        on_device, mesh=mesh, in_specs=in_specs, out_specs=out_specs, check_vma=False
    )
```

profile of v0, /device:TPU:2, one launch (start us, length us, event | category | flops | bytes accessed | tf_op | source)
XLA Modules:
  0.0 472.1 jit_solution(3480206786806552087)
XLA Ops:
  6.5 0.7 convert_bitcast_fusion
  7.3 0.1 copy.7
  7.4 0.2 mul.32
  7.6 0.4 mul.33
  8.0 0.6 copy-done.6
  8.6 2.0 fusion.10
  10.7 0.0 all-reduce.8.cloned.1.call-start
  10.7 0.7 copy-done.7
  11.5 92.9 %all-reduce.6.cloned.1.call-done = f32[512,512]{1,0:T(8,128)} async-done(((f32[512,512]{1,0:T(8,128)}), f32[512,512]{1,0:T(8,128)}) %all-reduce.6.cloned.1.call-update) | async-done | bytes 1048592 | tf_op jit(solution)/shard_map/psum | solution.py:46
  104.4 1.4 sub.38
  105.9 1.6 gather_fusion
  107.5 1.1 select_select_fusion.2
  108.7 0.0 all-reduce.10.cloned.1.call-start
  108.7 83.7 %all-reduce.8.cloned.1.call-done = f32[512,512]{1,0:T(8,128)} async-done(((f32[512,512]{1,0:T(8,128)}), f32[512,512]{1,0:T(8,128)}) %all-reduce.8.cloned.1.call-update) | async-done | bytes 1048592 | tf_op jit(solution)/shard_map/psum | solution.py:16
  192.4 3.6 fusion.2
  196.0 1.9 convolution_subtract_fusion.3
  197.9 1.9 fusion.8
  199.8 1.9 convolution_subtract_fusion.2
  201.7 3.2 broadcast_select_fusion.2
  204.9 0.0 all-reduce.10.cloned.1.call-update
  205.0 0.2 all-reduce.12.cloned.1.call-start
  205.2 77.8 %all-reduce.10.cloned.1.call-done = f32[512,512]{1,0:T(8,128)} async-done(((f32[512,512]{1,0:T(8,128)}), f32[512,512]{1,0:T(8,128)}) %all-reduce.10.cloned.1.call-update) | async-done | bytes 1048592 | tf_op jit(solution)/shard_map/psum | solution.py:16
  283.0 5.2 %broadcast_select_fusion.1 = (f32[512,512]{1,0:T(8,128)}, f32[512,512]{1,0:T(8,128)}) fusion(pred[]{:T(512)S(6)} %eq.44, f32[512,512]{1,0:T(8,128)} %get-tuple-element.46, f32[512,512]{1,0:T(8,128)} %copy-done.3, f32[512,512]{1,0:T(8,128)} %all-reduce.10.cloned.1.call-done, f32[512,512]{1,0:T(8,128)S(1)} %copy-done.1, pred[512]{0:T(512)(128)(4,1)S(1)} %fusion.36, ...), kind=kOutput, calls=%fused_computation.32 | convolution fusion | flops 1612709888 | bytes 7342082 | tf_op jit(solution)/shard_map/dot_general | solution.py:20
  288.3 0.0 all-reduce.14.cloned.1.call-start
  288.3 81.9 %all-reduce.12.cloned.1.call-done = f32[512,512]{1,0:T(8,128)} async-done(((f32[512,512]{1,0:T(8,128)}), f32[512,512]{1,0:T(8,128)}) %all-reduce.12.cloned.1.call-update) | async-done | bytes 1048592 | tf_op jit(solution)/shard_map/psum | solution.py:16
  370.2 2.0 fusion.4
  372.2 1.9 convolution_subtract_fusion.1
  374.1 1.9 fusion.9
  376.0 1.8 convolution_subtract_fusion
  377.9 3.2 broadcast_select_fusion
  381.1 79.7 %all-reduce.14.cloned.1.call-done = f32[512,512]{1,0:T(8,128)} async-done(((f32[512,512]{1,0:T(8,128)}), f32[512,512]{1,0:T(8,128)}) %all-reduce.14.cloned.1.call-update) | async-done | bytes 1048592 | tf_op jit(solution)/shard_map/psum | solution.py:16
  460.8 4.8 %select_select_fusion = f32[512,512]{1,0:T(8,128)} fusion(f32[512,512]{1,0:T(8,128)} %get-tuple-element.50, f32[512,512]{1,0:T(8,128)S(1)} %convolution_subtract_fusion, f32[512,512]{1,0:T(8,128)} %get-tuple-element.48, f32[512,512]{1,0:T(8,128)} %all-reduce.14.cloned.1.call-done, f32[512,512]{1,0:T(8,128)S(1)} %copy-done.2, ...), kind=kOutput, calls=%fused_computation.17 | convolution fusion | flops 1612185600 | bytes 6292993 | tf_op jit(solution)/shard_map/dot_general | solution.py:20
  (26 shorter events, 0.2 us)
Async XLA Ops:
  6.5 1.5 copy-start
  6.5 97.9 %all-reduce.6.cloned.1.call-start = ((), (), s32[]{:S(2)}) async-start(), calls=%async_computation | async-start | bytes 2097152 | tf_op jit(solution)/shard_map/psum | solution.py:46
  7.6 1.0 copy-start.6
  10.6 93.8 %copy-start.5 = (f32[512,512]{1,0:T(8,128)S(1)}, f32[512,512]{1,0:T(8,128)}, u32[]{:S(2)}) copy-start(f32[512,512]{1,0:T(8,128)} %param.13) | copy-start | bytes 3145732
  10.7 181.7 %all-reduce.8.cloned.1.call-start = ((), (), s32[]{:S(2)}) async-start(), calls=%async_computation.1 | async-start | bytes 2097152 | tf_op jit(solution)/shard_map/psum | solution.py:16
  10.7 0.8 copy-start.7
  108.7 174.4 %all-reduce.10.cloned.1.call-start = ((), (), s32[]{:S(2)}) async-start(), calls=%async_computation.2 | async-start | bytes 2097152 | tf_op jit(solution)/shard_map/psum | solution.py:16
  192.4 3.6 copy-start.1
  201.7 3.2 copy-start.3
  205.0 165.3 %all-reduce.12.cloned.1.call-start = ((), (), s32[]{:S(2)}) async-start(), calls=%async_computation.3 | async-start | bytes 2097152 | tf_op jit(solution)/shard_map/psum | solution.py:16
  288.3 172.5 %all-reduce.14.cloned.1.call-start = ((), (), s32[]{:S(2)}) async-start(), calls=%async_computation.4 | async-start | bytes 2097152 | tf_op jit(solution)/shard_map/psum | solution.py:16
  370.2 2.0 copy-start.2
  376.0 1.9 copy-start.4
Sparse Core Ops, SparseCore 0:
  10.8 93.6 all-reduce.5
  108.8 83.5 all-reduce.7
  205.1 77.9 all-reduce.9
  288.4 81.7 all-reduce.11
  381.2 79.5 all-reduce.13
where the time goes:
time: 472 us
  waiting for transfers between devices  416 us (88%)
  matrix products  35.3 us (7%)
  between operations  13.4 us (3%)
    psum x4, waiting for transfers between devices, spread(): return lax.psum(jnp.where(mine, value, jnp.zeros_like(value)), axis)  323 us
    psum x1, waiting for transfers between devices, on_device(): merged = front - lax.psum(partial_value, 'gz')  92.9 us
    dot_general x13, matrix products, product(): jnp.dot(first_matrix, second_matrix, precision=precise, preferred_element...  35.3 us
  transfers between devices with their start and end apart: 5, of which 5 were waited for; matrix products, arithmetic and copies ran while one was open for 0% of the time, Pallas kernels for 0%

commit v1 on v0

v1 whole, which is shorter than its diff:
```python
import functools

import jax
import jax.numpy as jnp
from jax import lax
from jax.experimental import pallas as pl
from jax.experimental.pallas import tpu as pltpu
from jax.sharding import PartitionSpec as P

BS = 128
NS_STEPS = 3
MESH = pl.DeviceIdType.MESH
ANY = pl.BlockSpec(memory_space=pl.ANY)


def remote(src, dst, send_sem, recv_sem, where):
    return pltpu.make_async_remote_copy(
        src_ref=src, dst_ref=dst, send_sem=send_sem, recv_sem=recv_sem,
        device_id=where, device_id_type=MESH,
    )


def greet(peers):
    barrier = pltpu.get_barrier_semaphore()
    for peer in peers:
        pl.semaphore_signal(barrier, inc=1, device_id=peer, device_id_type=MESH)
    pl.semaphore_wait(barrier, len(peers))


def gz_peers(n):
    me = lax.axis_index("gz")
    return [{"gz": lax.rem(me + k, n)} for k in range(1, n)]


def local_move(src, stage, dst, sems):
    inward = pltpu.make_async_copy(src, stage, sems.at[0])
    inward.start()
    inward.wait()
    outward = pltpu.make_async_copy(stage, dst, sems.at[1])
    outward.start()
    outward.wait()


def scatter_kernel(n, x, out, stage, send, recv, local):
    me = lax.axis_index("gz")
    greet(gz_peers(n))
    copies = []
    for k in range(1, n):
        peer = lax.rem(me + k, n)
        copy = remote(x.at[peer], out.at[me], send.at[k - 1], recv.at[k - 1], {"gz": peer})
        copy.start()
        copies.append(copy)
    local_move(x.at[me], stage, out.at[me], local)
    for copy in copies:
        copy.wait()


def gather_kernel(n, x, out, stage, send, recv, local):
    me = lax.axis_index("gz")
    greet(gz_peers(n))
    copies = []
    for k in range(1, n):
        peer = lax.rem(me + k, n)
        copy = remote(x, out.at[me], send.at[k - 1], recv.at[k - 1], {"gz": peer})
        copy.start()
        copies.append(copy)
    local_move(x, stage, out.at[me], local)
    for copy in copies:
        copy.wait()


def panel_rows_kernel(n, rows, x, out, stage, send, recv, row_send, row_recv,
                      pair_send, pair_recv, local):
    me = lax.axis_index("gz")
    row = lax.axis_index("row")
    core = lax.rem(row, 2)
    chip = row // 2
    chips = rows // 2
    partner = {"row": row + 1 - 2 * core}
    greet(
        gz_peers(n)
        + [{"row": lax.rem(row + 2 * k, rows)} for k in range(1, chips)]
        + [partner]
    )
    mine = out.at[core, me]
    down = [
        remote(x, mine, row_send.at[k - 1], row_recv, {"row": core + 2 * k})
        for k in range(1, chips)
    ]

    @pl.when(chip == 0)
    def _():
        for copy in down:
            copy.start()
        local_move(x, stage, mine, local)

    @pl.when(chip != 0)
    def _():
        down[0].wait_recv()

    across = []
    for k in range(1, n):
        copy = remote(mine, mine, send.at[k - 1], recv.at[k - 1], {"gz": lax.rem(me + k, n)})
        copy.start()
        across.append(copy)
    pairs = [remote(mine, mine, pair_send.at[0], pair_recv.at[0], partner)]
    pairs[0].start()
    for k in range(1, n):
        across[k - 1].wait_recv()
        landed = out.at[core, lax.rem(me - k + n, n)]
        copy = remote(landed, landed, pair_send.at[k], pair_recv.at[k], partner)
        copy.start()
        pairs.append(copy)
    for copy in pairs:
        copy.wait()
    for copy in across:
        copy.wait_send()

    @pl.when(chip == 0)
    def _():
        for copy in down:
            copy.wait_send()


def lower_kernel(n, cols, root, count, parts, x, *refs):
    spread = count > 1
    if spread:
        out, whole, stage, plus, minus, recv, send, gathered, local = refs
    else:
        out, stage, plus, minus, recv, local = refs
    me = lax.axis_index("gz")
    col = lax.axis_index("col")
    apart = lax.rem(col - root + cols, cols)
    far = cols // 2
    following = {"col": lax.rem(col + 1, cols)}
    preceding = {"col": lax.rem(col + cols - 1, cols)}
    greet((gz_peers(n) if spread else []) + [following, preceding])
    height = x.shape[1] // parts
    pieces = [(i, pl.ds(j * height, height)) for i in range(count) for j in range(parts)]

    def hop(index, source, sems, where):
        i, span = pieces[index]
        return remote(source.at[i, span], out.at[i, span], sems.at[index], recv.at[index], where)

    @pl.when(apart == 0)
    def _():
        for index in range(len(pieces)):
            hop(index, x, plus, following).start()
            hop(index, x, minus, preceding).start()
        local_move(x, stage, out, local)

    @pl.when(apart != 0)
    def _():
        for index in range(len(pieces)):
            hop(index, out, plus, following).wait_recv()

            @pl.when(apart < far)
            def _():
                hop(index, out, plus, following).start()

            @pl.when(apart > far + 1)
            def _():
                hop(index, out, minus, preceding).start()

            if spread and index == parts - 1:
                for k in range(1, n):
                    remote(out.at[0], whole.at[me], send.at[k - 1], gathered.at[k - 1],
                           {"gz": lax.rem(me + k, n)}).start()

    if spread:
        @pl.when(apart == 0)
        def _():
            for k in range(1, n):
                remote(out.at[0], whole.at[me], send.at[k - 1], gathered.at[k - 1],
                       {"gz": lax.rem(me + k, n)}).start()

        local_move(out.at[0], stage.at[0], whole.at[me], local)
        for k in range(1, n):
            remote(out.at[0], whole.at[me], send.at[k - 1], gathered.at[k - 1],
                   {"gz": lax.rem(me + k, n)}).wait()
    for index in range(len(pieces)):
        @pl.when(apart < far)
        def _():
            hop(index, out, plus, following).wait_send()

        @pl.when((apart == 0) | (apart > far + 1))
        def _():
            hop(index, out, minus, preceding).wait_send()


def call(kernel, outs, scratch, identity, *arguments):
    return pl.pallas_call(
        kernel,
        out_shape=outs,
        in_specs=[ANY] * len(arguments),
        out_specs=jax.tree.map(lambda _: ANY, outs),
        scratch_shapes=scratch,
        compiler_params=pltpu.CompilerParams(collective_id=identity, has_side_effects=True),
    )(*arguments)


def dma(*shape):
    return pltpu.SemaphoreType.DMA(shape)


def f32(*shape):
    return jax.ShapeDtypeStruct(shape, jnp.float32)


def product(first_matrix, second_matrix):
    return jnp.dot(
        first_matrix, second_matrix, precision=lax.Precision.HIGH,
        preferred_element_type=jnp.float32,
    )


def newton_inverse(pivot_block):
    block_width = pivot_block.shape[0]
    full_inverse = 2.0 * jnp.eye(block_width, dtype=jnp.float32) - pivot_block
    for iteration in range(NS_STEPS - 1):
        full_inverse = 2.0 * full_inverse - product(
            product(full_inverse, pivot_block), full_inverse
        )
    return full_inverse


def on_device(n, rows, cols, front, lower_parts, upper_parts, pattern, row_perm):
    width = front.shape[0]
    inner = lower_parts.shape[2]
    piece = width // n
    layer = lax.axis_index("gz")
    grid_row = lax.axis_index("row")
    grid_col = lax.axis_index("col")
    start = layer * piece
    order = row_perm[0]
    masked = lower_parts[0].reshape(width // BS, BS, inner // BS, BS)
    masked = masked * pattern[0].astype(jnp.float32)[:, None, :, None]
    masked = jnp.take(masked.reshape(width, inner), order, axis=0)
    partial_value = product(masked, upper_parts[0]).reshape(n, piece, width)
    own_front = jnp.take(front, lax.dynamic_slice(order, (start,), (piece,)), axis=0)

    slab = pltpu.VMEM((piece, width), jnp.float32)
    received = call(
        functools.partial(scatter_kernel, n), f32(n, piece, width),
        [slab, dma(n - 1), dma(n - 1), dma(2)], 0, partial_value,
    )
    own = own_front - jnp.sum(received, axis=0)

    panel_rows = call(
        functools.partial(panel_rows_kernel, n, rows), f32(2, n, piece, width),
        [slab, dma(n - 1), dma(n - 1), dma(rows // 2 - 1), dma(), dma(n), dma(n), dma(2)],
        1, own,
    ).reshape(2, width, width)
    first_row, second_row = panel_rows[0], panel_rows[1]

    inverse = newton_inverse(first_row)
    both = jnp.concatenate([lax.dynamic_slice(second_row, (start, 0), (piece, width)), own])
    lowers = product(both, inverse).reshape(2, piece, width)
    parts = 2
    pieces = 2 * parts
    lower, second_lower = call(
        functools.partial(lower_kernel, n, cols, 0, 2, parts),
        (f32(2, piece, width), f32(n, piece, width)),
        [pltpu.VMEM((2, piece, width), jnp.float32), dma(pieces), dma(pieces), dma(pieces),
         dma(n - 1), dma(n - 1), dma(2)],
        2, lowers,
    )
    second_row = second_row - product(second_lower.reshape(width, width), first_row)
    updated = own - product(lower[1], first_row)
    own_inverse = lax.dynamic_slice(inverse, (start, 0), (piece, width))
    replaced = jnp.where(grid_row == 0, own_inverse, lowers[1])
    own = jnp.where(grid_col == 0, replaced, jnp.where(grid_row == 0, own, updated))

    inverse = newton_inverse(second_row)
    lowers = product(own, inverse)
    parts = 4
    lower = call(
        functools.partial(lower_kernel, n, cols, 1, 1, parts), f32(1, piece, width),
        [pltpu.VMEM((1, piece, width), jnp.float32), dma(parts), dma(parts), dma(parts), dma(2)],
        3, lowers.reshape(1, piece, width),
    )
    updated = own - product(lower[0], second_row)
    own_inverse = lax.dynamic_slice(inverse, (start, 0), (piece, width))
    replaced = jnp.where(grid_row == 1, own_inverse, lowers)
    changed = jnp.where(grid_col == 1, replaced, jnp.where(grid_row == 1, own, updated))
    own = jnp.where((grid_row == 0) | (grid_col == 0), own, changed)

    factored = call(
        functools.partial(gather_kernel, n), f32(n, piece, width),
        [slab, dma(n - 1), dma(n - 1), dma(2)], 4, own,
    )
    return factored.reshape(width, width)


def solution(mesh):
    in_specs = (
        P("row", "col"),
        P("gz", "row", None),
        P("gz", None, "col"),
        P("gz", "row", None),
        P("row", None),
    )
    body = functools.partial(
        on_device, mesh.shape["gz"], mesh.shape["row"], mesh.shape["col"]
    )
    return jax.shard_map(
        body, mesh=mesh, in_specs=in_specs, out_specs=P("row", "col"), check_vma=False
    )
```

time: 472 us -> 135 us (0.29)
  the two profiles are of different devices: /device:TPU:2 before, /device:TPU:168 now
where the time goes in v1:
time: 135 us
  Pallas kernels  105 us (78%)
  matrix products  17.7 us (13%)
  other arithmetic  6.74 us (5%)
  local copies, waits for them, and re-layouts  5.52 us (4%)
    pallas_call x5, Pallas kernels, call(): pl.pallas_call(kernel, out_shape=outs, in_specs=[ANY] * len(arguments), o...  105 us
    dot_general x14, matrix products, product(): jnp.dot(first_matrix, second_matrix, precision=lax.Precision.HIGH, prefer...  17.7 us
    unnamed x14, local copies, waits for them, and re-layouts  2.81 us

profile of v1, /device:TPU:168, one launch (start us, length us, event | category | flops | bytes accessed | tf_op | source)
XLA Modules:
  0.0 134.8 jit_solution(4248635234325011461)
XLA Ops:
  0.0 0.8 convert_bitcast_fusion
  0.8 0.1 copy.7
  0.9 0.2 mul.36
  1.1 1.1 bitcast_multiply_fusion
  2.3 1.6 %gather_fusion.1 = f32[512,256]{1,0:T(8,128)S(1)} fusion(f32[512,256]{1,0:T(8,128)S(1)} %bitcast_multiply_fusion, s32[1024]{0:T(1024)S(1)} %pad_clamp_fusion), kind=kCustom, calls=%fused_computation.1 | custom fusion | bytes 1050624 | tf_op jit(solution)/shard_map/jit(_take)/gather | solution.py:238
  3.8 0.5 broadcast.168
  4.4 0.7 reduce.3
  5.2 0.1 broadcast_select_fusion
  5.3 1.6 %fusion.7.x = f32[8,64,512]{2,1,0:T(8,128)} fusion(f32[8,64,256]{2,1,0:T(8,128)S(1)} %bitcast.66, f32[1,256,512]{2,1,0:T(8,128)S(1)} %copy-done.4), kind=kOutput, calls=%fused_computation.22 | convolution fusion | flops 402653184 | bytes 2097152 | tf_op jit(solution)/shard_map/dot_general | solution.py:211
  6.9 18.9 %shard_map.55 = f32[8,64,512]{2,1,0:T(8,128)} custom-call(f32[8,64,512]{2,1,0:T(8,128)} %fusion.7.x), custom_call_target="tpu_custom_call" | custom-call | tf_op jit(solution)/shard_map/pallas_call | solution.py:192
  25.8 1.3 reduce_sum.9
  27.2 0.7 gather_fusion
  27.9 0.8 select_subtract_fusion.6.x
  28.7 31.0 %shard_map.56 = f32[2,8,64,512]{3,2,1,0:T(8,128)} custom-call(f32[64,512]{1,0:T(8,128)} %select_subtract_fusion.6.x), custom_call_target="tpu_custom_call" | custom-call | tf_op jit(solution)/shard_map/pallas_call | solution.py:192
  59.7 1.8 %fusion.30 = (f32[1,8,64,512]{3,2,1,0:T(8,128)S(1)}, f32[1,8,64,512]{3,2,1,0:T(8,128)S(1)}, f32[1,8,64,512]{3,2,1,0:T(8,128)S(1)}) fusion(f32[2,8,64,512]{3,2,1,0:T(8,128)} %shard_map.56, s32[8,64]{1,0:T(8,128)S(1)} %multiply_add_fusion), kind=kLoop, calls=%fused_computation.60 | loop fusion | flops 786432 | bytes 5244928 | tf_op jit(solution)/shard_map/slice | solution.py:254
  61.5 1.0 fusion.31
  62.6 1.0 convolution_subtract_fusion.4
  63.6 1.0 fusion.32
  64.6 1.0 convolution_subtract_fusion.3
  65.7 1.1 fusion.15
  66.8 28.4 %shard_map.57 = (f32[2,64,512]{2,1,0:T(8,128)}, f32[8,64,512]{2,1,0:T(8,128)}) custom-call(f32[2,64,512]{2,1,0:T(8,128)} %bitcast.67), custom_call_target="tpu_custom_call" | custom-call | tf_op jit(solution)/shard_map/pallas_call | solution.py:192
  95.2 1.5 %fusion.2 = f32[64,512]{1,0:T(8,128)S(1)} fusion(f32[64,512]{1,0:T(8,128)S(1)} %copy-done.3, f32[512,512]{1,0:T(8,128)S(1)} %bitcast.59, f32[128,512]{1,0:T(8,128)} %fusion.15, f32[2,64,512]{2,1,0:T(8,128)} %get-tuple-element.7, f32[512,512]{1,0:T(8,128)S(1)} %convolution_subtract_fusion.3, s32[]{:T(128)S(6)} %select_n.106, pred[]{:T(512)S(6)} %eq.31, ...), kind=kOutput, calls=%fused_computation.13 | convolution fusion | flops 100794368 | bytes 1703942 | tf_op jit(solution)/shard_map/dot_general | solution.py:211
  96.7 2.2 %convolution_subtract_fusion.2 = f32[512,512]{1,0:T(8,128)S(1)} fusion(f32[512,512]{1,0:T(8,128)S(1)} %bitcast.62, f32[512,512]{1,0:T(8,128)} %bitcast.69, f32[512,512]{1,0:T(8,128)S(1)} %bitcast.60), kind=kOutput, calls=%fused_computation.6 | convolution fusion | flops 805568512 | bytes 4194304 | tf_op jit(solution)/shard_map/dot_general | solution.py:211
  99.0 1.0 fusion.5
  100.0 1.0 convolution_subtract_fusion.1
  101.0 1.0 fusion.33
  102.0 1.0 convolution_subtract_fusion
  103.1 1.1 fusion.34
  104.1 13.2 %shard_map.58 = f32[1,64,512]{2,1,0:T(8,128)} custom-call(f32[1,64,512]{2,1,0:T(8,128)} %bitcast.68), custom_call_target="tpu_custom_call" | custom-call | tf_op jit(solution)/shard_map/pallas_call | solution.py:192
  117.4 2.1 %fusion.4.x = f32[64,512]{1,0:T(8,128)} fusion(f32[64,512]{1,0:T(8,128)S(1)} %fusion.2, f32[512,512]{1,0:T(8,128)S(1)} %convolution_subtract_fusion.2, f32[1,64,512]{2,1,0:T(8,128)} %shard_map.58, f32[64,512]{1,0:T(8,128)} %fusion.34, f32[512,512]{1,0:T(8,128)S(1)} %convolution_subtract_fusion, s32[]{:T(128)S(6)} %select_n.106, pred[]{:T(512)S(6)} %eq.36, ...), kind=kOutput, calls=%fused_computation.15 | convolution fusion | flops 100827136 | bytes 1703943 | tf_op jit(solution)/shard_map/dot_general | solution.py:211
  119.5 13.1 %shard_map.59 = f32[8,64,512]{2,1,0:T(8,128)} custom-call(f32[64,512]{1,0:T(8,128)} %fusion.4.x), custom_call_target="tpu_custom_call" | custom-call | tf_op jit(solution)/shard_map/pallas_call | solution.py:192
  132.5 2.3 %copy.11 = f32[512,512]{1,0:T(8,128)} copy(f32[512,512]{1,0:T(8,128)} %bitcast.64) | data formatting | bytes 2097152
  (22 shorter events, 0.4 us)
Async XLA Ops:
  0.0 27.2 %copy-start = (f32[512,512]{1,0:T(8,128)S(1)}, f32[512,512]{1,0:T(8,128)}, u32[]{:S(2)}) copy-start(f32[512,512]{1,0:T(8,128)} %param.5) | copy-start | bytes 3145732
  0.0 2.2 %copy-start.5 = (s32[1,512]{1,0:T(1,128)S(1)}, s32[1,512]{1,0:T(1,128)}, u32[]{:S(2)}) copy-start(s32[1,512]{1,0:T(1,128)} %param.9) | copy-start | bytes 6148
  2.2 3.1 %copy-start.4 = (f32[1,256,512]{2,1,0:T(8,128)S(1)}, f32[1,256,512]{2,1,0:T(8,128)}, u32[]{:S(2)}) copy-start(f32[1,256,512]{2,1,0:T(8,128)} %param.7) | copy-start | bytes 1572868
  61.5 4.1 %copy-start.1 = (f32[1,8,64,512]{3,2,1,0:T(8,128)}, f32[1,8,64,512]{3,2,1,0:T(8,128)S(1)}, u32[]{:S(2)}) copy-start(f32[1,8,64,512]{3,2,1,0:T(8,128)S(1)} %get-tuple-element.9) | copy-start | bytes 3145732
  64.6 1.1 copy-start.3
  95.2 1.5 %copy-start.2 = (f32[1,8,64,512]{3,2,1,0:T(8,128)S(1)}, f32[1,8,64,512]{3,2,1,0:T(8,128)}, u32[]{:S(2)}) copy-start(f32[1,8,64,512]{3,2,1,0:T(8,128)} %copy-done.1) | copy-start | bytes 3145732

commit v2 on v1

v2 whole, which is shorter than its diff:
```python
import functools

import jax
import jax.numpy as jnp
from jax import lax
from jax.experimental import pallas as pl
from jax.experimental.pallas import tpu as pltpu
from jax.sharding import PartitionSpec as P

BS = 128
NS_STEPS = 3
MESH = pl.DeviceIdType.MESH
ANY = pl.BlockSpec(memory_space=pl.ANY)


def remote(src, dst, send_sem, recv_sem, where):
    return pltpu.make_async_remote_copy(
        src_ref=src, dst_ref=dst, send_sem=send_sem, recv_sem=recv_sem,
        device_id=where, device_id_type=MESH,
    )


def greet(peers):
    barrier = pltpu.get_barrier_semaphore()
    for peer in peers:
        pl.semaphore_signal(barrier, inc=1, device_id=peer, device_id_type=MESH)
    pl.semaphore_wait(barrier, len(peers))


def gz_peers(n):
    me = lax.axis_index("gz")
    return [{"gz": lax.rem(me + k, n)} for k in range(1, n)]


def local_move(src, stage, dst, sems):
    inward = pltpu.make_async_copy(src, stage, sems.at[0])
    inward.start()
    inward.wait()
    outward = pltpu.make_async_copy(stage, dst, sems.at[1])
    outward.start()
    outward.wait()


def scatter_kernel(n, x, out, stage, send, recv, local):
    me = lax.axis_index("gz")
    greet(gz_peers(n))
    copies = []
    for k in range(1, n):
        peer = lax.rem(me + k, n)
        copy = remote(x.at[peer], out.at[me], send.at[k - 1], recv.at[k - 1], {"gz": peer})
        copy.start()
        copies.append(copy)
    local_move(x.at[me], stage, out.at[me], local)
    for copy in copies:
        copy.wait()


def ring_gather(n, rows, own, at, send, recv, begun=None, landed=None):
    me = lax.axis_index("gz")
    z = lax.rem(me, 2)
    flip = 1 - 2 * z
    left, right = lax.rem(me + n - 2, n), lax.rem(me + 2, n)
    over = lax.rem(me + n // 2, n)
    half, quarter = rows // 2, rows // 4
    to_right, to_left, to_pair = {"gz": right}, {"gz": left}, {"gz": me + flip}

    def own_part(which, low, size):
        return own(low, size)

    plan = [
        (own_part, me, 0, half, to_right),
        (own_part, me, half, half, to_right),
        (own_part, me, 0, half, to_left),
        (own_part, me, half, half, to_left),
        (own_part, me, 0, half, to_pair),
        (own_part, me, half, half, to_pair),
        (at, left, 0, half, to_right),
        (at, right, half, half, to_left),
        (at, left, half, half, to_pair),
        (at, right, half, half, to_pair),
        (at, over, half, half, to_pair),
        (at, me + flip, 0, half, to_right),
        (at, me + flip, 0, half, to_left),
        (at, left + flip, 0, quarter, to_right),
        (at, right + flip, quarter, quarter, to_left),
    ]
    copies = [
        remote(source(which, low, size), at(which, low, size), send.at[i], recv.at[i], where)
        for i, (source, which, low, size, where) in enumerate(plan)
    ]
    for i in (4, 0, 3, 5, 1, 2):
        copies[i].start()
    released = {4: (11, 12), 0: (6,), 3: (7, 9), 1: (8,), 7: (10,), 11: (13,), 12: (14,)}
    whole = {1: left, 2: right, 5: me + flip, 6: over, 8: left + flip, 9: right + flip}
    if begun is not None:
        begun()
    if landed is not None:
        landed(me)
    for i in (4, 0, 3, 1, 7, 11, 12, 2, 5, 6, 8, 9, 10, 13, 14):
        copies[i].wait_recv()
        for j in released.get(i, ()):
            copies[j].start()
        if landed is not None and i in whole:
            landed(whole[i])
    if landed is not None:
        landed(over + flip)
    for copy in copies:
        copy.wait_send()


def ring_peers(n):
    me = lax.axis_index("gz")
    return [
        {"gz": lax.rem(me + 2, n)},
        {"gz": lax.rem(me + n - 2, n)},
        {"gz": me + 1 - 2 * lax.rem(me, 2)},
    ]


STEPS = 15


def gather_kernel(n, x, out, stage, send, recv, local):
    me = lax.axis_index("gz")
    greet(ring_peers(n))
    ring_gather(
        n, x.shape[0], lambda low, size: x.at[pl.ds(low, size)],
        lambda which, low, size: out.at[which, pl.ds(low, size)], send, recv,
        begun=lambda: local_move(x, stage, out.at[me], local),
    )


def panel_rows_kernel(n, rows, x, out, stage, send, recv, row_send, row_recv,
                      pair_send, pair_recv, local):
    me = lax.axis_index("gz")
    row = lax.axis_index("row")
    core = lax.rem(row, 2)
    chip = row // 2
    chips = rows // 2
    partner = {"row": row + 1 - 2 * core}
    greet(
        ring_peers(n)
        + [{"row": lax.rem(row + 2 * k, rows)} for k in range(1, chips)]
        + [partner]
    )
    mine = out.at[core, me]
    down = [
        remote(x, mine, row_send.at[k - 1], row_recv, {"row": core + 2 * k})
        for k in range(1, chips)
    ]

    @pl.when(chip == 0)
    def _():
        for copy in down:
            copy.start()
        local_move(x, stage, mine, local)

    @pl.when(chip != 0)
    def _():
        down[0].wait_recv()

    pairs = []

    def landed(which):
        slab = out.at[core, which]
        k = len(pairs)
        copy = remote(slab, slab, pair_send.at[k], pair_recv.at[k], partner)
        copy.start()
        pairs.append(copy)

    at = lambda which, low, size: out.at[core, which, pl.ds(low, size)]
    ring_gather(
        n, x.shape[0], lambda low, size: at(me, low, size), at, send, recv, landed=landed
    )
    for copy in pairs:
        copy.wait()

    @pl.when(chip == 0)
    def _():
        for copy in down:
            copy.wait_send()


def lower_kernel(n, cols, root, height, spread, x, *refs):
    if spread:
        out, whole, stage, plus, minus, hop_recv, send, recv, pair_send, pair_recv, local = refs
    else:
        out, stage, plus, minus, hop_recv, local = refs
    me = lax.axis_index("gz")
    col = lax.axis_index("col")
    row = lax.axis_index("row")
    core = lax.rem(row, 2)
    partner = {"row": row + 1 - 2 * core}
    apart = lax.rem(col - root + cols, cols)
    far = cols // 2
    following = {"col": lax.rem(col + 1, cols)}
    preceding = {"col": lax.rem(col + cols - 1, cols)}
    greet((ring_peers(n) + [partner] if spread else []) + [following, preceding])
    count = x.shape[0] // height

    def hop(index, source, sems, where):
        span = pl.ds(index * height, height)
        return remote(source.at[span], out.at[span], sems.at[index], hop_recv.at[index], where)

    def pass_on(index):
        @pl.when(apart != 0)
        def _():
            hop(index, out, plus, following).wait_recv()

            @pl.when(apart < far)
            def _():
                hop(index, out, plus, following).start()

            @pl.when(apart > far + 1)
            def _():
                hop(index, out, minus, preceding).start()

    @pl.when(apart == 0)
    def _():
        for index in range(count):
            hop(index, x, plus, following).start()
            hop(index, x, minus, preceding).start()
        local_move(x, stage, out, local)

    if spread:
        pass_on(0)
        pairs = []
        at = lambda which, low, size: whole.at[which, pl.ds(core * height + low, size)]
        mine = at(me, 0, height)
        local_move(out.at[pl.ds(0, height)], stage.at[pl.ds(0, height)], mine, local)

        def begun():
            for index in range(1, count):
                pass_on(index)

        def landed(which):
            slab = at(which, 0, height)
            k = len(pairs)
            copy = remote(slab, slab, pair_send.at[k], pair_recv.at[k], partner)
            copy.start()
            pairs.append(copy)

        ring_gather(
            n, height, lambda low, size: out.at[pl.ds(low, size)], at, send, recv, begun, landed
        )
        for copy in pairs:
            copy.wait()
    else:
        for index in range(count):
            pass_on(index)
    for index in range(count):
        @pl.when(apart < far)
        def _():
            hop(index, out, plus, following).wait_send()

        @pl.when((apart == 0) | (apart > far + 1))
        def _():
            hop(index, out, minus, preceding).wait_send()


def call(kernel, outs, scratch, identity, *arguments):
    return pl.pallas_call(
        kernel,
        out_shape=outs,
        in_specs=[ANY] * len(arguments),
        out_specs=jax.tree.map(lambda _: ANY, outs),
        scratch_shapes=scratch,
        compiler_params=pltpu.CompilerParams(collective_id=identity, has_side_effects=True),
    )(*arguments)


def dma(*shape):
    return pltpu.SemaphoreType.DMA(shape)


def f32(*shape):
    return jax.ShapeDtypeStruct(shape, jnp.float32)


def product(first_matrix, second_matrix):
    return jnp.dot(
        first_matrix, second_matrix, precision=lax.Precision.HIGH,
        preferred_element_type=jnp.float32,
    )


def times_inverse(stacked, pivot_block):
    residual = jnp.eye(pivot_block.shape[0], dtype=jnp.float32) - pivot_block
    for step in range(NS_STEPS):
        stacked = stacked + product(stacked, residual)
        if step < NS_STEPS - 1:
            residual = product(residual, residual)
    return stacked


def on_device(n, rows, cols, front, lower_parts, upper_parts, pattern, row_perm):
    width = front.shape[0]
    inner = lower_parts.shape[2]
    piece = width // n
    layer = lax.axis_index("gz")
    grid_row = lax.axis_index("row")
    grid_col = lax.axis_index("col")
    start = layer * piece
    order = row_perm[0]
    masked = lower_parts[0].reshape(width // BS, BS, inner // BS, BS)
    masked = masked * pattern[0].astype(jnp.float32)[:, None, :, None]
    masked = jnp.take(masked.reshape(width, inner), order, axis=0)
    partial_value = product(masked, upper_parts[0]).reshape(n, piece, width)
    own_front = jnp.take(front, lax.dynamic_slice(order, (start,), (piece,)), axis=0)

    slab = pltpu.VMEM((piece, width), jnp.float32)
    received = call(
        functools.partial(scatter_kernel, n), f32(n, piece, width),
        [slab, dma(n - 1), dma(n - 1), dma(2)], 0, partial_value,
    )
    own = own_front - jnp.sum(received, axis=0)

    panel_rows = call(
        functools.partial(panel_rows_kernel, n, rows), f32(2, n, piece, width),
        [slab, dma(STEPS), dma(STEPS), dma(rows // 2 - 1), dma(), dma(n), dma(n), dma(2)],
        1, own,
    ).reshape(2, width, width)
    first_row, second_row = panel_rows[0], panel_rows[1]
    unit = (jnp.arange(piece)[:, None] + start == jnp.arange(width)[None, :]).astype(jnp.float32)

    half = piece // 2
    shared = lax.dynamic_slice(
        second_row, (start + half * lax.rem(grid_row, 2), 0), (half, width)
    )
    lowers = times_inverse(jnp.concatenate([shared, own, unit]), first_row)
    own_inverse = lowers[half + piece :]
    lowers = lowers[: half + piece]
    count = 3
    lower, second_lower = call(
        functools.partial(lower_kernel, n, cols, 0, half, True),
        (f32(half + piece, width), f32(n, piece, width)),
        [pltpu.VMEM((half + piece, width), jnp.float32), dma(count), dma(count), dma(count),
         dma(STEPS), dma(STEPS), dma(n), dma(n), dma(2)],
        2, lowers,
    )
    second_row = second_row - product(second_lower.reshape(width, width), first_row)
    updated = own - product(lower[half:], first_row)
    replaced = jnp.where(grid_row == 0, own_inverse, lowers[half:])
    own = jnp.where(grid_col == 0, replaced, jnp.where(grid_row == 0, own, updated))

    lowers = times_inverse(jnp.concatenate([own, unit]), second_row)
    own_inverse = lowers[piece:]
    lowers = lowers[:piece]
    count = 4
    lower = call(
        functools.partial(lower_kernel, n, cols, 1, piece // count, False), f32(piece, width),
        [slab, dma(count), dma(count), dma(count), dma(2)],
        3, lowers,
    )
    updated = own - product(lower, second_row)
    replaced = jnp.where(grid_row == 1, own_inverse, lowers)
    changed = jnp.where(grid_col == 1, replaced, jnp.where(grid_row == 1, own, updated))
    own = jnp.where((grid_row == 0) | (grid_col == 0), own, changed)

    factored = call(
        functools.partial(gather_kernel, n), f32(n, piece, width),
        [slab, dma(STEPS), dma(STEPS), dma(2)], 4, own,
    )
    return factored.reshape(width, width)


def solution(mesh):
    in_specs = (
        P("row", "col"),
        P("gz", "row", None),
        P("gz", None, "col"),
        P("gz", "row", None),
        P("row", None),
    )
    body = functools.partial(
        on_device, mesh.shape["gz"], mesh.shape["row"], mesh.shape["col"]
    )
    return jax.shard_map(
        body, mesh=mesh, in_specs=in_specs, out_specs=P("row", "col"), check_vma=False
    )
```

time: 135 us -> 140 us (1.037)
  Pallas kernels: 105 us -> 110 us
  matrix products: 17.7 us -> 14 us
  local copies, waits for them, and re-layouts: 5.52 us -> 7.7 us
    pallas_call x5, Pallas kernels: 105 us -> 110 us  [call(): pl.pallas_call(kernel, out_shape=outs, in_specs=[ANY] * len(arguments), o...]
    dot_general x14, matrix products: 17.7 us -> 14 us  [product(): jnp.dot(first_matrix, second_matrix, precision=lax.Precision.HIGH, prefer...]
    sub x0 -> x1, other arithmetic: none -> 2.81 us  [times_inverse(): residual = jnp.eye(pivot_block.shape[0], dtype=jnp.float32) - pivot_block]
    slice x1 -> x0, other arithmetic: 1.79 us -> none  [on_device(): first_row, second_row = (panel_rows[0], panel_rows[1])]
    unnamed x14 -> x12, local copies, waits for them, and re-layouts: 2.81 us -> 2.8 us
where the time goes in v2:
time: 140 us
  Pallas kernels  110 us (79%)
  matrix products  14 us (10%)
  other arithmetic  7.83 us (6%)
  local copies, waits for them, and re-layouts  7.7 us (6%)
    pallas_call x5, Pallas kernels, call(): pl.pallas_call(kernel, out_shape=outs, in_specs=[ANY] * len(arguments), o...  110 us
    dot_general x14, matrix products, product(): jnp.dot(first_matrix, second_matrix, precision=lax.Precision.HIGH, prefer...  14 us
    sub x1, other arithmetic, times_inverse(): residual = jnp.eye(pivot_block.shape[0], dtype=jnp.float32) - pivot_block  2.81 us

profile of v2, /device:TPU:168, one launch (start us, length us, event | category | flops | bytes accessed | tf_op | source)
XLA Modules:
  0.0 139.8 jit_solution(2548245476777981726)
XLA Ops:
  0.0 0.8 convert_bitcast_fusion
  1.1 1.1 bitcast_multiply_fusion
  2.3 1.6 %gather_fusion.1 = f32[512,256]{1,0:T(8,128)S(1)} fusion(f32[512,256]{1,0:T(8,128)S(1)} %bitcast_multiply_fusion, s32[1024]{0:T(1024)S(1)} %pad_clamp_fusion), kind=kCustom, calls=%fused_computation.1 | custom fusion | bytes 1050624 | tf_op jit(solution)/shard_map/jit(_take)/gather | solution.py:307
  3.8 0.5 broadcast.123
  4.4 0.7 reduce.3
  5.3 1.6 %fusion.6.x = f32[8,64,512]{2,1,0:T(8,128)} fusion(f32[8,64,256]{2,1,0:T(8,128)S(1)} %bitcast.55, f32[1,256,512]{2,1,0:T(8,128)S(1)} %copy-done.3), kind=kOutput, calls=%fused_computation.23 | convolution fusion | flops 402653184 | bytes 2097152 | tf_op jit(solution)/shard_map/dot_general | solution.py:281
  6.9 18.9 %shard_map.55 = f32[8,64,512]{2,1,0:T(8,128)} custom-call(f32[8,64,512]{2,1,0:T(8,128)} %fusion.6.x), custom_call_target="tpu_custom_call" | custom-call | tf_op jit(solution)/shard_map/pallas_call | solution.py:262
  25.8 1.3 reduce_sum.9
  27.2 0.7 gather_fusion
  27.9 0.7 select_subtract_fusion.x
  28.7 30.3 %shard_map.56 = f32[2,8,64,512]{3,2,1,0:T(8,128)} custom-call(f32[64,512]{1,0:T(8,128)} %select_subtract_fusion.x), custom_call_target="tpu_custom_call" | custom-call | tf_op jit(solution)/shard_map/pallas_call | solution.py:262
  59.0 2.8 %convert_subtract_fusion.3 = (f32[1,8,64,512]{3,2,1,0:T(8,128)S(1)}, f32[1,8,64,512]{3,2,1,0:T(8,128)S(1)}, f32[1,8,64,512]{3,2,1,0:T(8,128)}) fusion(s32[8,64]{1,0:T(8,128)S(1)} %multiply_add_fusion, f32[2,8,64,512]{3,2,1,0:T(8,128)} %shard_map.56), kind=kLoop, calls=%fused_computation.18 | loop fusion | flops 786432 | bytes 5244928 | tf_op jit(solution)/shard_map/sub | solution.py:288
  61.9 0.8 constant_dynamic-slice_fusion
  62.7 0.5 convolution_add_fusion.2
  63.3 1.0 fusion.21
  64.3 0.5 convolution_add_fusion.1
  64.8 1.0 fusion.22
  65.8 0.5 convolution_add_fusion
  66.2 0.7 slice.41.x
  66.9 29.9 %shard_map.57 = (f32[96,512]{1,0:T(8,128)}, f32[8,64,512]{2,1,0:T(8,128)}) custom-call(f32[96,512]{1,0:T(8,128)} %slice.41.x), custom_call_target="tpu_custom_call" | custom-call | tf_op jit(solution)/shard_map/pallas_call | solution.py:262
  96.9 1.4 %fusion.2 = f32[64,512]{1,0:T(8,128)S(1)} fusion(f32[64,512]{1,0:T(8,128)S(1)} %copy-done.1, f32[512,512]{1,0:T(8,128)S(1)} %bitcast.48, f32[160,512]{1,0:T(8,128)S(1)} %convolution_add_fusion, f32[96,512]{1,0:T(8,128)} %get-tuple-element.7, pred[]{:T(512)S(6)} %eq.45, pred[]{:T(512)S(6)} %eq.46), kind=kOutput, calls=%fused_computation.15 | convolution fusion | flops 100794368 | bytes 1703938 | tf_op jit(solution)/shard_map/dot_general | solution.py:281
  98.3 2.2 %convolution_subtract_fusion = f32[512,512]{1,0:T(8,128)S(1)} fusion(f32[512,512]{1,0:T(8,128)} %bitcast.52, f32[512,512]{1,0:T(8,128)S(1)} %bitcast.56, f32[512,512]{1,0:T(8,128)S(1)} %bitcast.49), kind=kOutput, calls=%fused_computation.4 | convolution fusion | flops 805568512 | bytes 4194304 | tf_op jit(solution)/shard_map/dot_general | solution.py:281
  100.6 0.5 convolution_add_fusion.5
  101.0 1.0 fusion.5
  102.1 0.4 convolution_add_fusion.4
  102.5 1.0 fusion.23
  103.5 0.4 convolution_add_fusion.3
  103.9 0.7 slice.43.x
  104.6 15.3 %shard_map.58 = f32[64,512]{1,0:T(8,128)} custom-call(f32[64,512]{1,0:T(8,128)} %slice.43.x), custom_call_target="tpu_custom_call" | custom-call | tf_op jit(solution)/shard_map/pallas_call | solution.py:262
  119.9 2.0 %fusion.4.x = f32[64,512]{1,0:T(8,128)} fusion(f32[64,512]{1,0:T(8,128)S(1)} %fusion.2, f32[64,512]{1,0:T(8,128)} %shard_map.58, f32[512,512]{1,0:T(8,128)S(1)} %convolution_subtract_fusion, f32[128,512]{1,0:T(8,128)S(1)} %convolution_add_fusion.3, pred[]{:T(512)S(6)} %eq.53, pred[]{:T(512)S(6)} %eq.52, pred[]{:T(512)S(6)} %or.3), kind=kOutput, calls=%fused_computation.17 | convolution fusion | flops 100827136 | bytes 1703939 | tf_op jit(solution)/shard_map/dot_general | solution.py:281
  121.9 15.6 %shard_map.59 = f32[8,64,512]{2,1,0:T(8,128)} custom-call(f32[64,512]{1,0:T(8,128)} %fusion.4.x), custom_call_target="tpu_custom_call" | custom-call | tf_op jit(solution)/shard_map/pallas_call | solution.py:262
  137.5 2.3 %copy.11 = f32[512,512]{1,0:T(8,128)} copy(f32[512,512]{1,0:T(8,128)} %bitcast.53) | data formatting | bytes 2097152
  (24 shorter events, 0.9 us)
Async XLA Ops:
  0.0 27.2 %copy-start = (f32[512,512]{1,0:T(8,128)S(1)}, f32[512,512]{1,0:T(8,128)}, u32[]{:S(2)}) copy-start(f32[512,512]{1,0:T(8,128)} %param.5) | copy-start | bytes 3145732
  0.0 2.2 %copy-start.4 = (s32[1,512]{1,0:T(1,128)S(1)}, s32[1,512]{1,0:T(1,128)}, u32[]{:S(2)}) copy-start(s32[1,512]{1,0:T(1,128)} %param.9) | copy-start | bytes 6148
  2.2 3.1 %copy-start.3 = (f32[1,256,512]{2,1,0:T(8,128)S(1)}, f32[1,256,512]{2,1,0:T(8,128)}, u32[]{:S(2)}) copy-start(f32[1,256,512]{2,1,0:T(8,128)} %param.7) | copy-start | bytes 1572868
  59.0 3.8 %copy-start.1 = (f32[64,512]{1,0:T(8,128)S(1)}, f32[64,512]{1,0:T(8,128)}, u32[]{:S(2)}) copy-start(f32[64,512]{1,0:T(8,128)} %select_subtract_fusion.x) | copy-start | bytes 393220
  96.9 1.4 %copy-start.2 = (f32[8,64,512]{2,1,0:T(8,128)S(1)}, f32[8,64,512]{2,1,0:T(8,128)}, u32[]{:S(2)}) copy-start(f32[8,64,512]{2,1,0:T(8,128)} %get-tuple-element.8) | copy-start | bytes 3145732

commit v3 on v0

v3 whole, which is shorter than its diff:
```python
import functools

import jax
import jax.numpy as jnp
from jax import lax
from jax.experimental import pallas as pl
from jax.experimental.pallas import tpu as pltpu
from jax.sharding import PartitionSpec as P

BS = 128
NS_STEPS = 3
MESH = pl.DeviceIdType.MESH
F32 = jnp.float32


def dot(first_matrix, second_matrix):
    return jnp.dot(first_matrix, second_matrix, preferred_element_type=F32)


def split(value):
    high = value.astype(jnp.bfloat16)
    return high, (value - high.astype(F32)).astype(jnp.bfloat16)


def product(first_pair, second_pair):
    return (
        dot(first_pair[0], second_pair[0])
        + dot(first_pair[0], second_pair[1])
        + dot(first_pair[1], second_pair[0])
    )


def unit_rows(count, width, start):
    down = lax.broadcasted_iota(jnp.int32, (count, width), 0) + start
    return jnp.where(down == lax.broadcasted_iota(jnp.int32, (count, width), 1), 1.0, 0.0)


def times_inverse(stacked, pivot_block):
    residual = unit_rows(*pivot_block.shape, 0) - pivot_block
    for step in range(NS_STEPS):
        parts = split(residual)
        stacked = stacked + product(split(stacked), parts)
        if step < NS_STEPS - 1:
            residual = product(parts, parts)
    return stacked


class Link:
    def __init__(self, send, recv):
        self.send, self.recv, self.sent, self.got = send, recv, 0, 0

    def batch(self, sends, receives):
        first = self.sent, self.got
        self.sent += sends
        self.got += receives

        def copy(src, dst, send_index, recv_index, where):
            return pltpu.make_async_remote_copy(
                src_ref=src, dst_ref=dst, send_sem=self.send.at[first[0] + send_index],
                recv_sem=self.recv.at[first[1] + recv_index],
                device_id=where, device_id_type=MESH,
            )

        return copy


def front_kernel(n, rows, cols, order, pattern, front, lower, upper, out,
                 onehot, masked, part, arrived, own, panel, lows, low_in, inverse, shared,
                 own_next, second, lows_next, low_next_in, inverse_next, own_last, send, recv):
    me, row, col = lax.axis_index("gz"), lax.axis_index("row"), lax.axis_index("col")
    core = lax.rem(row, 2)
    partner = {"row": row + 1 - 2 * core}
    width = front.shape[0]
    piece = width // n
    half = piece // 2
    link = Link(send, recv)
    across = [lax.rem(me + k, n) for k in range(1, n)]
    behind = [lax.rem(me + n - k, n) for k in range(1, n)]

    barrier = pltpu.get_barrier_semaphore()
    peers = (
        [{"gz": peer} for peer in across]
        + [{"row": lax.rem(row + k, rows)} for k in range(1, rows)]
        + [{"col": lax.rem(col + k, cols)} for k in range(1, cols)]
    )
    for peer in peers:
        pl.semaphore_signal(barrier, inc=1, device_id=peer, device_id_type=MESH)

    for i in range(width // BS):
        for j in range(lower.shape[1] // BS):
            block = (slice(i * BS, (i + 1) * BS), slice(j * BS, (j + 1) * BS))
            masked[block] = lower[block] * pattern[i, j].astype(F32)
    onehot[...] = jnp.where(
        order[...] == lax.broadcasted_iota(jnp.int32, (width, width), 1), 1.0, 0.0
    ).astype(jnp.bfloat16)
    picks = onehot[...]
    ordered = [dot(picks, value).astype(jnp.bfloat16) for value in split(masked[...])]
    part[...] = product(ordered, split(upper[...])).reshape(n, piece, width)
    chosen = onehot[pl.ds(pl.multiple_of(me * piece, piece), piece), :]
    high = front[...].astype(jnp.bfloat16)
    rest = front[...] - high.astype(F32)
    middle, low = split(rest)
    own_front = dot(chosen, high) + dot(chosen, middle) + dot(chosen, low)

    pl.semaphore_wait(barrier, len(peers))
    copy = link.batch(n - 1, n - 1)
    scatter = [
        copy(part.at[peer], arrived.at[me], k, k, {"gz": peer}) for k, peer in enumerate(across)
    ]
    for item in scatter:
        item.start()
    own_front = own_front - part[me]
    for k, item in enumerate(scatter):
        item.wait_recv()
        own_front = own_front - arrived[behind[k]]
    own[...] = own_front

    def span(which):
        return pl.ds(pl.multiple_of(which * half, half), half)

    mine = span(core)
    downs = []
    for p in range(2):
        copy = link.batch(rows - 1, 1)
        down = []
        for j in range(1, rows):
            target = lax.rem(row + j, rows)
            there = span(lax.rem(target, 2))
            down.append(
                copy(own.at[there], panel.at[p, me, there], j - 1, 0, {"row": target})
            )
        downs.append(down)

        @pl.when(row == p)
        def _():
            for item in down:
                item.start()
            panel[p, me, mine] = own[mine]

    gathers, pairs = [], []
    for p in range(2):
        @pl.when(row != p)
        def _():
            downs[p][0].wait_recv()

        copy = link.batch(n - 1, n - 1)
        slab = panel.at[p, me, mine]
        gathers.append([copy(slab, slab, k, k, {"gz": peer}) for k, peer in enumerate(across)])
        copy = link.batch(n, n)
        slabs = [panel.at[p, slot, mine] for slot in [me] + behind]
        pairs.append([copy(slab, slab, k, k, partner) for k, slab in enumerate(slabs)])
        for item in gathers[p]:
            item.start()
        pairs[p][0].start()

    def finish(gather, pair):
        for k, item in enumerate(gather):
            item.wait_recv()
            pair[k + 1].start()
        for item in pair:
            item.wait_recv()

    finish(gathers[0], pairs[0])
    own_start = me * piece

    def column_copies(count_root, source, landing, pieces):
        copies = []
        for low, size in pieces:
            copy = link.batch(cols - 1, 1)
            window = pl.ds(low, size)
            copies.append([
                copy(source.at[window], landing.at[window], k - 1, 0,
                     {"col": lax.rem(col + k, cols)})
                for k in range(1, cols)
            ])
        return copies

    middle_out = sorted(range(cols - 1), key=lambda k: abs(2 * k + 2 - cols))
    firsts = column_copies(0, lows, low_in, [(0, half), (half, piece)])

    @pl.when(col == 0)
    def _():
        stacked = jnp.concatenate(
            [panel[1, me, mine], own[...], unit_rows(piece, width, own_start)]
        )
        solved = times_inverse(stacked, panel[0].reshape(width, width))
        lows[...] = solved[: half + piece]
        low_in[...] = solved[: half + piece]
        inverse[...] = solved[half + piece :]
        for group in firsts:
            for k in middle_out:
                group[k].start()

    finish(gathers[1], pairs[1])

    @pl.when(col != 0)
    def _():
        firsts[0][0].wait_recv()

    copy = link.batch(n - 1, n - 1)
    lower_gather = [
        copy(low_in.at[pl.ds(0, half)], shared.at[me, mine], k, k, {"gz": peer})
        for k, peer in enumerate(across)
    ]
    for item in lower_gather:
        item.start()
    copy = link.batch(n, n)
    lower_pair = [copy(low_in.at[pl.ds(0, half)], shared.at[me, mine], 0, 0, partner)]
    lower_pair += [
        copy(shared.at[slot, mine], shared.at[slot, mine], k + 1, k + 1, partner)
        for k, slot in enumerate(behind)
    ]
    lower_pair[0].start()
    shared[me, mine] = low_in[pl.ds(0, half), :]

    @pl.when(col != 0)
    def _():
        firsts[1][0].wait_recv()

    @pl.when((col == 0) & (row == 0))
    def _():
        own_next[...] = inverse[...]

    @pl.when((col == 0) & (row != 0))
    def _():
        own_next[...] = lows[pl.ds(half, piece), :]

    @pl.when((col != 0) & (row == 0))
    def _():
        own_next[...] = own[...]

    @pl.when((col != 0) & (row != 0))
    def _():
        own_next[...] = own[...] - product(
            split(low_in[pl.ds(half, piece), :]), split(panel[0].reshape(width, width))
        )

    finish(lower_gather, lower_pair)
    [nexts] = column_copies(1, lows_next, low_next_in, [(0, piece)])

    @pl.when(col != 0)
    def _():
        second[...] = panel[1].reshape(width, width) - product(
            split(shared[...].reshape(width, width)), split(panel[0].reshape(width, width))
        )

    @pl.when(col == 1)
    def _():
        stacked = jnp.concatenate([own_next[...], unit_rows(piece, width, own_start)])
        solved = times_inverse(stacked, second[...])
        lows_next[...] = solved[:piece]
        low_next_in[...] = solved[:piece]
        inverse_next[...] = solved[piece:]
        for k in middle_out:
            nexts[k].start()

    @pl.when(col != 1)
    def _():
        nexts[0].wait_recv()

    @pl.when((col == 0) | (row == 0) | ((col > 1) & (row == 1)))
    def _():
        own_last[...] = own_next[...]

    @pl.when((col == 1) & (row == 1))
    def _():
        own_last[...] = inverse_next[...]

    @pl.when((col == 1) & (row > 1))
    def _():
        own_last[...] = lows_next[...]

    @pl.when((col > 1) & (row > 1))
    def _():
        own_last[...] = own_next[...] - product(split(low_next_in[...]), split(second[...]))

    copy = link.batch(n - 1, n - 1)
    final = [copy(own_last, out.at[me], k, k, {"gz": peer}) for k, peer in enumerate(across)]
    for item in final:
        item.start()
    out[me] = own_last[...]
    for item in final:
        item.wait_recv()

    for group in [scatter, final, lower_gather, lower_pair] + gathers + pairs:
        for item in group:
            item.wait_send()
    for p in range(2):
        @pl.when(row == p)
        def _():
            for item in downs[p]:
                item.wait_send()

    @pl.when(col == 0)
    def _():
        for group in firsts:
            for item in group:
                item.wait_send()

    @pl.when(col == 1)
    def _():
        for item in nexts:
            item.wait_send()


def on_device(n, rows, cols, front, lower_parts, upper_parts, pattern, row_perm):
    width = front.shape[0]
    inner = lower_parts.shape[2]
    piece = width // n
    half = piece // 2
    in_vmem = pl.BlockSpec(memory_space=pltpu.VMEM)
    in_smem = pl.BlockSpec(memory_space=pltpu.SMEM)

    def room(*shape, dtype=F32):
        return pltpu.VMEM(shape, dtype)

    factored = pl.pallas_call(
        functools.partial(front_kernel, n, rows, cols),
        out_shape=jax.ShapeDtypeStruct((n, piece, width), F32),
        in_specs=[in_vmem, in_smem, in_vmem, in_vmem, in_vmem],
        out_specs=in_vmem,
        scratch_shapes=[
            room(width, width, dtype=jnp.bfloat16),
            room(width, inner),
            room(n, piece, width),
            room(n, piece, width),
            room(piece, width),
            room(2, n, piece, width),
            room(half + piece, width),
            room(half + piece, width),
            room(piece, width),
            room(n, piece, width),
            room(piece, width),
            room(width, width),
            room(piece, width),
            room(piece, width),
            room(piece, width),
            room(piece, width),
            pltpu.SemaphoreType.DMA((128,)),
            pltpu.SemaphoreType.DMA((96,)),
        ],
        compiler_params=pltpu.CompilerParams(collective_id=0, has_side_effects=True),
    )(
        row_perm.reshape(width, 1), pattern[0], front, lower_parts[0], upper_parts[0],
    )
    return factored.reshape(width, width)


def solution(mesh):
    in_specs = (
        P("row", "col"),
        P("gz", "row", None),
        P("gz", None, "col"),
        P("gz", "row", None),
        P("row", None),
    )
    body = functools.partial(
        on_device, mesh.shape["gz"], mesh.shape["row"], mesh.shape["col"]
    )
    return jax.shard_map(
        body, mesh=mesh, in_specs=in_specs, out_specs=P("row", "col"), check_vma=False
    )
```

time: 472 us -> 106 us (0.22)
  the two profiles are of different devices: /device:TPU:2 before, /device:TPU:128 now
where the time goes in v3:
time: 106 us
  Pallas kernels  101 us (95%)
  local copies, waits for them, and re-layouts  4.45 us (4%)
    pallas_call x1, Pallas kernels, on_device(): pl.pallas_call(functools.partial(front_kernel, n, rows, cols), out_shape=...  101 us
    unnamed x5, local copies, waits for them, and re-layouts  2.94 us

profile of v3, /device:TPU:128, one launch (start us, length us, event | category | flops | bytes accessed | tf_op | source)
XLA Modules:
  0.0 105.5 jit_solution(17608121509822207867)
XLA Ops:
  0.0 0.0 copy-start.1
  0.0 0.0 copy-start
  0.0 0.7 copy-done.1
  0.7 0.6 copy.8.pattern
  1.3 0.0 copy-done
  1.3 0.9 copy.7.order
  2.2 101.0 %shard_map.55 = f32[8,64,512]{2,1,0:T(8,128)} custom-call(s32[512,1]{1,0:T(8,128)} %copy.7.order, s32[4,2]{1,0:T(4,128)} %copy.8.pattern, f32[512,512]{1,0:T(8,128)} %front.1, f32[512,256]{1,0:T(8,128)} %bitcast.6, f32[256,512]{1,0:T(8,128)} %bitcast.7), custom_call_target="tpu_custom_call" | custom-call | tf_op jit(solution)/shard_map/pallas_call | solution.py:317
  103.2 2.3 %copy.10 = f32[512,512]{1,0:T(8,128)} copy(f32[512,512]{1,0:T(8,128)} %bitcast.5) | data formatting | bytes 2097152
Async XLA Ops:
  0.0 0.7 copy-start.1
  0.0 1.3 %copy-start = (s32[1,512]{1,0:T(1,128)S(1)}, s32[1,512]{1,0:T(1,128)}, u32[]{:S(2)}) copy-start(s32[1,512]{1,0:T(1,128)} %param.9) | copy-start | bytes 6148

commit v4 on v3

--- a/solution.py
+++ b/solution.py
@@ -66,7 +66,7 @@
 
 def front_kernel(n, rows, cols, order, pattern, front, lower, upper, out,
                  onehot, masked, part, arrived, own, panel, lows, low_in, inverse, shared,
-                 own_next, second, lows_next, low_next_in, inverse_next, own_last, send, recv):
+                 own_next, second, second_high, second_low, lows_next, low_next_in, inverse_next, own_last, send, recv):
     me, row, col = lax.axis_index("gz"), lax.axis_index("row"), lax.axis_index("col")
     core = lax.rem(row, 2)
     partner = {"row": row + 1 - 2 * core}
@@ -119,7 +119,7 @@
         return pl.ds(pl.multiple_of(which * half, half), half)
 
     mine = span(core)
-    downs = []
+    downs, gathers, pairs = [], [], []
     for p in range(2):
         copy = link.batch(rows - 1, 1)
         down = []
@@ -130,28 +130,32 @@
                 copy(own.at[there], panel.at[p, me, there], j - 1, 0, {"row": target})
             )
         downs.append(down)
-
-        @pl.when(row == p)
-        def _():
-            for item in down:
-                item.start()
-            panel[p, me, mine] = own[mine]
-
-    gathers, pairs = [], []
-    for p in range(2):
-        @pl.when(row != p)
-        def _():
-            downs[p][0].wait_recv()
-
         copy = link.batch(n - 1, n - 1)
         slab = panel.at[p, me, mine]
         gathers.append([copy(slab, slab, k, k, {"gz": peer}) for k, peer in enumerate(across)])
         copy = link.batch(n, n)
         slabs = [panel.at[p, slot, mine] for slot in [me] + behind]
         pairs.append([copy(slab, slab, k, k, partner) for k, slab in enumerate(slabs)])
+
+    def descend(p):
+        @pl.when(row == p)
+        def _():
+            for item in downs[p]:
+                item.start()
+            panel[p, me, mine] = own[mine]
+
+        @pl.when(row != p)
+        def _():
+            downs[p][0].wait_recv()
+
+    def spread(p):
         for item in gathers[p]:
             item.start()
         pairs[p][0].start()
+
+    descend(0)
+    spread(0)
+    descend(1)
 
     def finish(gather, pair):
         for k, item in enumerate(gather):
@@ -161,22 +165,56 @@
             item.wait_recv()
 
     finish(gathers[0], pairs[0])
+    spread(1)
     own_start = me * piece
 
-    def column_copies(count_root, source, landing, pieces):
-        copies = []
-        for low, size in pieces:
-            copy = link.batch(cols - 1, 1)
-            window = pl.ds(low, size)
-            copies.append([
-                copy(source.at[window], landing.at[window], k - 1, 0,
-                     {"col": lax.rem(col + k, cols)})
-                for k in range(1, cols)
-            ])
-        return copies
-
-    middle_out = sorted(range(cols - 1), key=lambda k: abs(2 * k + 2 - cols))
-    firsts = column_copies(0, lows, low_in, [(0, half), (half, piece)])
+    def column_chain(root, source, landing, size):
+        apart = lax.rem(col - root + cols, cols)
+        far = cols // 2
+        following = {"col": lax.rem(col + 1, cols)}
+        preceding = {"col": lax.rem(col + cols - 1, cols)}
+        count = source.shape[0] // size
+        copy = link.batch(2 * count, count)
+
+        def hop(index, origin, ahead):
+            window = pl.ds(index * size, size)
+            return copy(
+                origin.at[window], landing.at[window], index + (0 if ahead else count), index,
+                following if ahead else preceding,
+            )
+
+        def begin():
+            for index in range(count):
+                hop(index, source, True).start()
+                hop(index, source, False).start()
+
+        def relay(index):
+            @pl.when(apart != 0)
+            def _():
+                hop(index, landing, True).wait_recv()
+
+            @pl.when((apart != 0) & (apart < far))
+            def _():
+                hop(index, landing, True).start()
+
+            @pl.when(apart > far + 1)
+            def _():
+                hop(index, landing, False).start()
+
+        def end():
+            @pl.when(apart < far)
+            def _():
+                for index in range(count):
+                    hop(index, landing, True).wait_send()
+
+            @pl.when((apart == 0) | (apart > far + 1))
+            def _():
+                for index in range(count):
+                    hop(index, landing, False).wait_send()
+
+        return begin, relay, end, count
+
+    begin, relay, end_first, count = column_chain(0, lows, low_in, half // 2)
 
     @pl.when(col == 0)
     def _():
@@ -187,15 +225,10 @@
         lows[...] = solved[: half + piece]
         low_in[...] = solved[: half + piece]
         inverse[...] = solved[half + piece :]
-        for group in firsts:
-            for k in middle_out:
-                group[k].start()
-
-    finish(gathers[1], pairs[1])
-
-    @pl.when(col != 0)
-    def _():
-        firsts[0][0].wait_recv()
+        begin()
+
+    relay(0)
+    relay(1)
 
     copy = link.batch(n - 1, n - 1)
     lower_gather = [
@@ -213,9 +246,9 @@
     lower_pair[0].start()
     shared[me, mine] = low_in[pl.ds(0, half), :]
 
-    @pl.when(col != 0)
-    def _():
-        firsts[1][0].wait_recv()
+    for index in range(2, count):
+        relay(index)
+    finish(gathers[1], pairs[1])
 
     @pl.when((col == 0) & (row == 0))
     def _():
@@ -236,7 +269,7 @@
         )
 
     finish(lower_gather, lower_pair)
-    [nexts] = column_copies(1, lows_next, low_next_in, [(0, piece)])
+    begin, relay, end_next, count = column_chain(1, lows_next, low_next_in, piece // 4)
 
     @pl.when(col != 0)
     def _():
@@ -251,33 +284,44 @@
         lows_next[...] = solved[:piece]
         low_next_in[...] = solved[:piece]
         inverse_next[...] = solved[piece:]
-        for k in middle_out:
-            nexts[k].start()
-
-    @pl.when(col != 1)
-    def _():
-        nexts[0].wait_recv()
-
-    @pl.when((col == 0) | (row == 0) | ((col > 1) & (row == 1)))
-    def _():
-        own_last[...] = own_next[...]
-
-    @pl.when((col == 1) & (row == 1))
-    def _():
-        own_last[...] = inverse_next[...]
-
-    @pl.when((col == 1) & (row > 1))
-    def _():
-        own_last[...] = lows_next[...]
-
-    @pl.when((col > 1) & (row > 1))
-    def _():
-        own_last[...] = own_next[...] - product(split(low_next_in[...]), split(second[...]))
-
-    copy = link.batch(n - 1, n - 1)
-    final = [copy(own_last, out.at[me], k, k, {"gz": peer}) for k, peer in enumerate(across)]
-    for item in final:
-        item.start()
+        begin()
+
+    @pl.when(col > 1)
+    def _():
+        second_high[...], second_low[...] = split(second[...])
+
+    final = []
+    for index in range(count):
+        relay(index)
+        size = piece // count
+        window = pl.ds(index * size, size)
+
+        @pl.when((col == 0) | (row == 0) | ((col > 1) & (row == 1)))
+        def _():
+            own_last[window] = own_next[window]
+
+        @pl.when((col == 1) & (row == 1))
+        def _():
+            own_last[window] = inverse_next[window]
+
+        @pl.when((col == 1) & (row > 1))
+        def _():
+            own_last[window] = lows_next[window]
+
+        @pl.when((col > 1) & (row > 1))
+        def _():
+            own_last[window] = own_next[window] - product(
+                split(low_next_in[window]), (second_high[...], second_low[...])
+            )
+
+        copy = link.batch(n - 1, n - 1)
+        items = [
+            copy(own_last.at[window], out.at[me, window], k, k, {"gz": peer})
+            for k, peer in enumerate(across)
+        ]
+        for item in items:
+            item.start()
+        final += items
     out[me] = own_last[...]
     for item in final:
         item.wait_recv()
@@ -291,16 +335,8 @@
             for item in downs[p]:
                 item.wait_send()
 
-    @pl.when(col == 0)
-    def _():
-        for group in firsts:
-            for item in group:
-                item.wait_send()
-
-    @pl.when(col == 1)
-    def _():
-        for item in nexts:
-            item.wait_send()
+    end_first()
+    end_next()
 
 
 def on_device(n, rows, cols, front, lower_parts, upper_parts, pattern, row_perm):
@@ -332,12 +368,14 @@
             room(n, piece, width),
             room(piece, width),
             room(width, width),
-            room(piece, width),
-            room(piece, width),
-            room(piece, width),
-            room(piece, width),
-            pltpu.SemaphoreType.DMA((128,)),
-            pltpu.SemaphoreType.DMA((96,)),
+            room(width, width, dtype=jnp.bfloat16),
+            room(width, width, dtype=jnp.bfloat16),
+            room(piece, width),
+            room(piece, width),
+            room(piece, width),
+            room(piece, width),
+            pltpu.SemaphoreType.DMA((144,)),
+            pltpu.SemaphoreType.DMA((112,)),
         ],
         compiler_params=pltpu.CompilerParams(collective_id=0, has_side_effects=True),
     )(

time: 106 us -> 91.1 us (0.86)
  the two profiles are of different devices: /device:TPU:128 before, /device:TPU:168 now
where the time goes in v4:
time: 91.1 us; the launch traced here: 90.9 us
  Pallas kernels  86.4 us (95%)
  local copies, waits for them, and re-layouts  4.45 us (5%)
    pallas_call x1, Pallas kernels, on_device(): pl.pallas_call(functools.partial(front_kernel, n, rows, cols), out_shape=...  86.4 us
    unnamed x5, local copies, waits for them, and re-layouts  2.94 us

profile of v4, /device:TPU:168, one launch (start us, length us, event | category | flops | bytes accessed | tf_op | source)
XLA Modules:
  0.0 90.9 jit_solution(17482953116484297536)
XLA Ops:
  0.0 0.0 copy-start.1
  0.0 0.0 copy-start
  0.0 0.7 copy-done.1
  0.7 0.6 copy.8.pattern
  1.3 0.0 copy-done
  1.3 0.9 copy.7.order
  2.2 86.4 %shard_map.55 = f32[8,64,512]{2,1,0:T(8,128)} custom-call(s32[512,1]{1,0:T(8,128)} %copy.7.order, s32[4,2]{1,0:T(4,128)} %copy.8.pattern, f32[512,512]{1,0:T(8,128)} %front.1, f32[512,256]{1,0:T(8,128)} %bitcast.6, f32[256,512]{1,0:T(8,128)} %bitcast.7), custom_call_target="tpu_custom_call" | custom-call | tf_op jit(solution)/shard_map/pallas_call | solution.py:353
  88.6 2.3 %copy.10 = f32[512,512]{1,0:T(8,128)} copy(f32[512,512]{1,0:T(8,128)} %bitcast.5) | data formatting | bytes 2097152
Async XLA Ops:
  0.0 0.7 copy-start.1
  0.0 1.3 %copy-start = (s32[1,512]{1,0:T(1,128)S(1)}, s32[1,512]{1,0:T(1,128)}, u32[]{:S(2)}) copy-start(s32[1,512]{1,0:T(1,128)} %param.9) | copy-start | bytes 6148

commit v5 on v4

--- a/solution.py
+++ b/solution.py
@@ -65,7 +65,7 @@
 
 
 def front_kernel(n, rows, cols, order, pattern, front, lower, upper, out,
-                 onehot, masked, part, arrived, own, panel, lows, low_in, inverse, shared,
+                 onehot, masked, part, base, arrived, own, panel, lows, low_in, inverse, shared,
                  own_next, second, second_high, second_low, lows_next, low_next_in, inverse_next, own_last, send, recv):
     me, row, col = lax.axis_index("gz"), lax.axis_index("row"), lax.axis_index("col")
     core = lax.rem(row, 2)
@@ -89,9 +89,10 @@
     for i in range(width // BS):
         for j in range(lower.shape[1] // BS):
             block = (slice(i * BS, (i + 1) * BS), slice(j * BS, (j + 1) * BS))
-            masked[block] = lower[block] * pattern[i, j].astype(F32)
+            masked[block] = lower[block] * pattern[pl.ds(j, 1), pl.ds(i, 1)].astype(F32)
+    sources = jnp.transpose(jnp.broadcast_to(order[...], (BS, width)))[:, :1]
     onehot[...] = jnp.where(
-        order[...] == lax.broadcasted_iota(jnp.int32, (width, width), 1), 1.0, 0.0
+        sources == lax.broadcasted_iota(jnp.int32, (width, width), 1), 1.0, 0.0
     ).astype(jnp.bfloat16)
     picks = onehot[...]
     ordered = [dot(picks, value).astype(jnp.bfloat16) for value in split(masked[...])]
@@ -100,36 +101,45 @@
     high = front[...].astype(jnp.bfloat16)
     rest = front[...] - high.astype(F32)
     middle, low = split(rest)
-    own_front = dot(chosen, high) + dot(chosen, middle) + dot(chosen, low)
+    base[...] = (
+        dot(chosen, high) + dot(chosen, middle) + dot(chosen, low) - part[me]
+    )
 
     pl.semaphore_wait(barrier, len(peers))
     copy = link.batch(n - 1, n - 1)
     scatter = [
         copy(part.at[peer], arrived.at[me], k, k, {"gz": peer}) for k, peer in enumerate(across)
     ]
-    for item in scatter:
-        item.start()
-    own_front = own_front - part[me]
-    for k, item in enumerate(scatter):
-        item.wait_recv()
-        own_front = own_front - arrived[behind[k]]
-    own[...] = own_front
+
+    def reduce():
+        for item in scatter:
+            item.start()
+        total = base[...]
+        for k, item in enumerate(scatter):
+            item.wait_recv()
+            total = total - arrived[behind[k]]
+        own[...] = total
+
+    pl.when(row != 1)(reduce)
 
     def span(which):
         return pl.ds(pl.multiple_of(which * half, half), half)
 
     mine = span(core)
-    downs, gathers, pairs = [], [], []
+    chip, chips = row // 2, rows // 2
+    downs, relays, gathers, pairs = [], [], [], []
     for p in range(2):
-        copy = link.batch(rows - 1, 1)
+        copy = link.batch(6, 1)
         down = []
-        for j in range(1, rows):
-            target = lax.rem(row + j, rows)
-            there = span(lax.rem(target, 2))
-            down.append(
-                copy(own.at[there], panel.at[p, me, there], j - 1, 0, {"row": target})
-            )
+        for j, target in enumerate((1 - p, 2, 3, rows - 2, rows - 1)):
+            there = span(target % 2)
+            down.append(copy(own.at[there], panel.at[p, me, there], j, 0, {"row": target}))
         downs.append(down)
+        slab = panel.at[p, me, mine]
+        relays.append([
+            copy(slab, slab, 5, 0, {"row": lax.rem(row + step, rows)})
+            for step in (2, rows - 2)
+        ])
         copy = link.batch(n - 1, n - 1)
         slab = panel.at[p, me, mine]
         gathers.append([copy(slab, slab, k, k, {"gz": peer}) for k, peer in enumerate(across)])
@@ -148,6 +158,14 @@
         def _():
             downs[p][0].wait_recv()
 
+        @pl.when((chip > 0) & (chip < chips // 2))
+        def _():
+            relays[p][0].start()
+
+        @pl.when(chip > chips // 2 + 1)
+        def _():
+            relays[p][1].start()
+
     def spread(p):
         for item in gathers[p]:
             item.start()
@@ -155,6 +173,7 @@
 
     descend(0)
     spread(0)
+    pl.when(row == 1)(reduce)
     descend(1)
 
     def finish(gather, pair):
@@ -335,8 +354,16 @@
             for item in downs[p]:
                 item.wait_send()
 
+        @pl.when((chip > 0) & (chip != chips // 2) & (chip != chips // 2 + 1))
+        def _():
+            relays[p][0].wait_send()
+
     end_first()
     end_next()
+
+
+def place_kernel(gathered, out):
+    out[...] = gathered[...]
 
 
 def on_device(n, rows, cols, front, lower_parts, upper_parts, pattern, row_perm):
@@ -345,7 +372,6 @@
     piece = width // n
     half = piece // 2
     in_vmem = pl.BlockSpec(memory_space=pltpu.VMEM)
-    in_smem = pl.BlockSpec(memory_space=pltpu.SMEM)
 
     def room(*shape, dtype=F32):
         return pltpu.VMEM(shape, dtype)
@@ -353,12 +379,13 @@
     factored = pl.pallas_call(
         functools.partial(front_kernel, n, rows, cols),
         out_shape=jax.ShapeDtypeStruct((n, piece, width), F32),
-        in_specs=[in_vmem, in_smem, in_vmem, in_vmem, in_vmem],
+        in_specs=[in_vmem] * 5,
         out_specs=in_vmem,
         scratch_shapes=[
             room(width, width, dtype=jnp.bfloat16),
             room(width, inner),
             room(n, piece, width),
+            room(piece, width),
             room(n, piece, width),
             room(piece, width),
             room(2, n, piece, width),
@@ -379,9 +406,14 @@
         ],
         compiler_params=pltpu.CompilerParams(collective_id=0, has_side_effects=True),
     )(
-        row_perm.reshape(width, 1), pattern[0], front, lower_parts[0], upper_parts[0],
-    )
-    return factored.reshape(width, width)
+        row_perm, pattern[0].T, front, lower_parts[0], upper_parts[0],
+    )
+    return pl.pallas_call(
+        place_kernel,
+        out_shape=jax.ShapeDtypeStruct((width, width), F32),
+        in_specs=[in_vmem],
+        out_specs=in_vmem,
+    )(factored.reshape(width, width))
 
 
 def solution(mesh):

time: 91.1 us -> 89.5 us (0.982)
  the two profiles are of different devices: /device:TPU:168 before, /device:TPU:296 now
where the time goes in v5:
time: 89.5 us; the launch traced here: 89.3 us
  Pallas kernels  89.3 us (100%)
    pallas_call x1, Pallas kernels, on_device(): pl.pallas_call(functools.partial(front_kernel, n, rows, cols), out_shape=...  87.1 us
    pallas_call x1, Pallas kernels, on_device(): pl.pallas_call(place_kernel, out_shape=jax.ShapeDtypeStruct((width, width...  2.26 us

profile of v5, /device:TPU:296, one launch (start us, length us, event | category | flops | bytes accessed | tf_op | source)
XLA Modules:
  0.0 89.3 jit_solution(1459073687756807875)
XLA Ops:
  0.0 87.1 %shard_map.55 = f32[8,64,512]{2,1,0:T(8,128)} custom-call(s32[1,512]{1,0:T(1,128)} %order.1, s32[2,4]{1,0:T(2,128)} %bitcast.9, f32[512,512]{1,0:T(8,128)} %front.1, f32[512,256]{1,0:T(8,128)} %bitcast.7, f32[256,512]{1,0:T(8,128)} %bitcast.8), custom_call_target="tpu_custom_call" | custom-call | tf_op jit(solution)/shard_map/pallas_call | solution.py:379
  87.1 2.3 %shard_map.56 = f32[512,512]{1,0:T(8,128)} custom-call(f32[512,512]{1,0:T(8,128)} %bitcast.6), custom_call_target="tpu_custom_call" | custom-call | tf_op jit(solution)/shard_map/pallas_call | solution.py:411

commit v6 on v5

--- a/solution.py
+++ b/solution.py
@@ -35,13 +35,18 @@
     return jnp.where(down == lax.broadcasted_iota(jnp.int32, (count, width), 1), 1.0, 0.0)
 
 
-def times_inverse(stacked, pivot_block):
+def powers(pivot_block):
     residual = unit_rows(*pivot_block.shape, 0) - pivot_block
-    for step in range(NS_STEPS):
-        parts = split(residual)
-        stacked = stacked + product(split(stacked), parts)
-        if step < NS_STEPS - 1:
-            residual = product(parts, parts)
+    squares = [residual]
+    for step in range(NS_STEPS - 1):
+        parts = split(squares[-1])
+        squares.append(product(parts, parts))
+    return squares
+
+
+def times_factors(stacked, squares):
+    for residual in squares:
+        stacked = stacked + product(split(stacked), split(residual))
     return stacked
 
 
@@ -65,7 +70,7 @@
 
 
 def front_kernel(n, rows, cols, order, pattern, front, lower, upper, out,
-                 onehot, masked, part, base, arrived, own, panel, lows, low_in, inverse, shared,
+                 onehot, masked, part, base, arrived, own, panel, squares, lows, low_in, inverse, shared,
                  own_next, second, second_high, second_low, lows_next, low_next_in, inverse_next, own_last, send, recv):
     me, row, col = lax.axis_index("gz"), lax.axis_index("row"), lax.axis_index("col")
     core = lax.rem(row, 2)
@@ -127,19 +132,21 @@
 
     mine = span(core)
     chip, chips = row // 2, rows // 2
-    downs, relays, gathers, pairs = [], [], [], []
+    downs, gathers, pairs = [], [], []
     for p in range(2):
-        copy = link.batch(6, 1)
+        copy = link.batch(rows, 1)
+        targets = (1, 2, 3, rows - 2, rows - 1) if p == 0 else (0, *range(2, rows))
         down = []
-        for j, target in enumerate((1 - p, 2, 3, rows - 2, rows - 1)):
+        for j, target in enumerate(targets):
             there = span(target % 2)
             down.append(copy(own.at[there], panel.at[p, me, there], j, 0, {"row": target}))
         downs.append(down)
         slab = panel.at[p, me, mine]
-        relays.append([
-            copy(slab, slab, 5, 0, {"row": lax.rem(row + step, rows)})
-            for step in (2, rows - 2)
-        ])
+        if p == 0:
+            relays = [
+                copy(slab, slab, rows - 1, 0, {"row": lax.rem(row + step, rows)})
+                for step in (2, rows - 2)
+            ]
         copy = link.batch(n - 1, n - 1)
         slab = panel.at[p, me, mine]
         gathers.append([copy(slab, slab, k, k, {"gz": peer}) for k, peer in enumerate(across)])
@@ -147,34 +154,31 @@
         slabs = [panel.at[p, slot, mine] for slot in [me] + behind]
         pairs.append([copy(slab, slab, k, k, partner) for k, slab in enumerate(slabs)])
 
-    def descend(p):
-        @pl.when(row == p)
-        def _():
-            for item in downs[p]:
-                item.start()
-            panel[p, me, mine] = own[mine]
-
-        @pl.when(row != p)
-        def _():
-            downs[p][0].wait_recv()
-
-        @pl.when((chip > 0) & (chip < chips // 2))
-        def _():
-            relays[p][0].start()
-
-        @pl.when(chip > chips // 2 + 1)
-        def _():
-            relays[p][1].start()
+    def leave(p):
+        for item in downs[p]:
+            item.start()
+        panel[p, me, mine] = own[mine]
+
+    def land(p):
+        pl.when(row != p)(downs[p][0].wait_recv)
 
     def spread(p):
         for item in gathers[p]:
             item.start()
         pairs[p][0].start()
 
-    descend(0)
+    pl.when(row == 0)(functools.partial(leave, 0))
+    land(0)
+    upward = (chip > 0) & (chip < chips // 2)
+    downward = chip > chips // 2 + 1
+    pl.when(upward)(relays[0].start)
+    pl.when(downward)(relays[1].start)
     spread(0)
-    pl.when(row == 1)(reduce)
-    descend(1)
+
+    @pl.when(row == 1)
+    def _():
+        reduce()
+        leave(1)
 
     def finish(gather, pair):
         for k, item in enumerate(gather):
@@ -184,6 +188,13 @@
             item.wait_recv()
 
     finish(gathers[0], pairs[0])
+
+    @pl.when(col == 0)
+    def _():
+        for step, residual in enumerate(powers(panel[0].reshape(width, width))):
+            squares[step] = residual
+
+    land(1)
     spread(1)
     own_start = me * piece
 
@@ -240,7 +251,7 @@
         stacked = jnp.concatenate(
             [panel[1, me, mine], own[...], unit_rows(piece, width, own_start)]
         )
-        solved = times_inverse(stacked, panel[0].reshape(width, width))
+        solved = times_factors(stacked, [squares[step] for step in range(NS_STEPS)])
         lows[...] = solved[: half + piece]
         low_in[...] = solved[: half + piece]
         inverse[...] = solved[half + piece :]
@@ -299,7 +310,7 @@
     @pl.when(col == 1)
     def _():
         stacked = jnp.concatenate([own_next[...], unit_rows(piece, width, own_start)])
-        solved = times_inverse(stacked, second[...])
+        solved = times_factors(stacked, powers(second[...]))
         lows_next[...] = solved[:piece]
         low_next_in[...] = solved[:piece]
         inverse_next[...] = solved[piece:]
@@ -354,9 +365,7 @@
             for item in downs[p]:
                 item.wait_send()
 
-        @pl.when((chip > 0) & (chip != chips // 2) & (chip != chips // 2 + 1))
-        def _():
-            relays[p][0].wait_send()
+    pl.when(upward | downward)(relays[0].wait_send)
 
     end_first()
     end_next()
@@ -389,6 +398,7 @@
             room(n, piece, width),
             room(piece, width),
             room(2, n, piece, width),
+            room(NS_STEPS, width, width),
             room(half + piece, width),
             room(half + piece, width),
             room(piece, width),
@@ -411,8 +421,9 @@
     return pl.pallas_call(
         place_kernel,
         out_shape=jax.ShapeDtypeStruct((width, width), F32),
-        in_specs=[in_vmem],
-        out_specs=in_vmem,
+        grid=(4,),
+        in_specs=[pl.BlockSpec((width // 4, width), lambda i: (i, 0))],
+        out_specs=pl.BlockSpec((width // 4, width), lambda i: (i, 0)),
     )(factored.reshape(width, width))
 
 

time: 89.5 us -> 87.9 us (0.982)
  the two profiles are of different devices: /device:TPU:296 before, /device:TPU:168 now
where the time goes in v6:
time: 87.9 us; the launch traced here: 87.7 us
  Pallas kernels  87.7 us (100%)
    pallas_call x1, Pallas kernels, on_device(): pl.pallas_call(functools.partial(front_kernel, n, rows, cols), out_shape=...  84.3 us
    pallas_call x1, Pallas kernels, on_device(): pl.pallas_call(place_kernel, out_shape=jax.ShapeDtypeStruct((width, width...  3.37 us

profile of v6, /device:TPU:168, one launch (start us, length us, event | category | flops | bytes accessed | tf_op | source)
XLA Modules:
  0.0 87.7 jit_solution(4018145006759142493)
XLA Ops:
  0.0 84.3 %shard_map.55 = f32[8,64,512]{2,1,0:T(8,128)} custom-call(s32[1,512]{1,0:T(1,128)} %order.1, s32[2,4]{1,0:T(2,128)} %bitcast.9, f32[512,512]{1,0:T(8,128)} %front.1, f32[512,256]{1,0:T(8,128)} %bitcast.7, f32[256,512]{1,0:T(8,128)} %bitcast.8), custom_call_target="tpu_custom_call" | custom-call | tf_op jit(solution)/shard_map/pallas_call | solution.py:388
  84.3 3.4 %shard_map.56 = f32[512,512]{1,0:T(8,128)} custom-call(f32[512,512]{1,0:T(8,128)} %bitcast.6), custom_call_target="tpu_custom_call" | custom-call | tf_op jit(solution)/shard_map/pallas_call | solution.py:421

commit v7 on v6

--- a/solution.py
+++ b/solution.py
@@ -70,7 +70,7 @@
 
 
 def front_kernel(n, rows, cols, order, pattern, front, lower, upper, out,
-                 onehot, masked, part, base, arrived, own, panel, squares, lows, low_in, inverse, shared,
+                 onehot, masked, part, base, arrived, own, panel, squares, lows, low_in, inverse,
                  own_next, second, second_high, second_low, lows_next, low_next_in, inverse_next, own_last, send, recv):
     me, row, col = lax.axis_index("gz"), lax.axis_index("row"), lax.axis_index("col")
     core = lax.rem(row, 2)
@@ -132,7 +132,7 @@
 
     mine = span(core)
     chip, chips = row // 2, rows // 2
-    downs, gathers, pairs = [], [], []
+    downs = []
     for p in range(2):
         copy = link.batch(rows, 1)
         targets = (1, 2, 3, rows - 2, rows - 1) if p == 0 else (0, *range(2, rows))
@@ -147,12 +147,14 @@
                 copy(slab, slab, rows - 1, 0, {"row": lax.rem(row + step, rows)})
                 for step in (2, rows - 2)
             ]
+
+    def exchange(block):
         copy = link.batch(n - 1, n - 1)
-        slab = panel.at[p, me, mine]
-        gathers.append([copy(slab, slab, k, k, {"gz": peer}) for k, peer in enumerate(across)])
+        slab = block.at[me, mine]
+        gather = [copy(slab, slab, k, k, {"gz": peer}) for k, peer in enumerate(across)]
         copy = link.batch(n, n)
-        slabs = [panel.at[p, slot, mine] for slot in [me] + behind]
-        pairs.append([copy(slab, slab, k, k, partner) for k, slab in enumerate(slabs)])
+        slabs = [block.at[slot, mine] for slot in [me] + behind]
+        return gather, [copy(slab, slab, k, k, partner) for k, slab in enumerate(slabs)]
 
     def leave(p):
         for item in downs[p]:
@@ -162,10 +164,10 @@
     def land(p):
         pl.when(row != p)(downs[p][0].wait_recv)
 
-    def spread(p):
-        for item in gathers[p]:
+    def spread(gather, pair):
+        for item in gather:
             item.start()
-        pairs[p][0].start()
+        pair[0].start()
 
     pl.when(row == 0)(functools.partial(leave, 0))
     land(0)
@@ -173,7 +175,8 @@
     downward = chip > chips // 2 + 1
     pl.when(upward)(relays[0].start)
     pl.when(downward)(relays[1].start)
-    spread(0)
+    gather, pair = exchange(panel.at[0])
+    spread(gather, pair)
 
     @pl.when(row == 1)
     def _():
@@ -187,7 +190,7 @@
         for item in pair:
             item.wait_recv()
 
-    finish(gathers[0], pairs[0])
+    finish(gather, pair)
 
     @pl.when(col == 0)
     def _():
@@ -195,7 +198,6 @@
             squares[step] = residual
 
     land(1)
-    spread(1)
     own_start = me * piece
 
     def column_chain(root, source, landing, size):
@@ -260,25 +262,14 @@
     relay(0)
     relay(1)
 
-    copy = link.batch(n - 1, n - 1)
-    lower_gather = [
-        copy(low_in.at[pl.ds(0, half)], shared.at[me, mine], k, k, {"gz": peer})
-        for k, peer in enumerate(across)
-    ]
-    for item in lower_gather:
-        item.start()
-    copy = link.batch(n, n)
-    lower_pair = [copy(low_in.at[pl.ds(0, half)], shared.at[me, mine], 0, 0, partner)]
-    lower_pair += [
-        copy(shared.at[slot, mine], shared.at[slot, mine], k + 1, k + 1, partner)
-        for k, slot in enumerate(behind)
-    ]
-    lower_pair[0].start()
-    shared[me, mine] = low_in[pl.ds(0, half), :]
+    second[me, mine] = panel[1, me, mine] - product(
+        split(low_in[pl.ds(0, half), :]), split(panel[0].reshape(width, width))
+    )
+    next_gather, next_pair = exchange(second)
+    spread(next_gather, next_pair)
 
     for index in range(2, count):
         relay(index)
-    finish(gathers[1], pairs[1])
 
     @pl.when((col == 0) & (row == 0))
     def _():
@@ -298,19 +289,13 @@
             split(low_in[pl.ds(half, piece), :]), split(panel[0].reshape(width, width))
         )
 
-    finish(lower_gather, lower_pair)
+    finish(next_gather, next_pair)
     begin, relay, end_next, count = column_chain(1, lows_next, low_next_in, piece // 4)
 
-    @pl.when(col != 0)
-    def _():
-        second[...] = panel[1].reshape(width, width) - product(
-            split(shared[...].reshape(width, width)), split(panel[0].reshape(width, width))
-        )
-
     @pl.when(col == 1)
     def _():
         stacked = jnp.concatenate([own_next[...], unit_rows(piece, width, own_start)])
-        solved = times_factors(stacked, powers(second[...]))
+        solved = times_factors(stacked, powers(second[...].reshape(width, width)))
         lows_next[...] = solved[:piece]
         low_next_in[...] = solved[:piece]
         inverse_next[...] = solved[piece:]
@@ -318,7 +303,7 @@
 
     @pl.when(col > 1)
     def _():
-        second_high[...], second_low[...] = split(second[...])
+        second_high[...], second_low[...] = split(second[...].reshape(width, width))
 
     final = []
     for index in range(count):
@@ -356,7 +341,7 @@
     for item in final:
         item.wait_recv()
 
-    for group in [scatter, final, lower_gather, lower_pair] + gathers + pairs:
+    for group in [scatter, gather, pair, next_gather, next_pair, final]:
         for item in group:
             item.wait_send()
     for p in range(2):
@@ -371,8 +356,23 @@
     end_next()
 
 
-def place_kernel(gathered, out):
-    out[...] = gathered[...]
+def place_kernel(count, gathered, out, stage, into, back):
+    size = gathered.shape[0] // count
+    windows = [pl.ds(i * size, size) for i in range(count)]
+    arrivals = [
+        pltpu.make_async_copy(gathered.at[w], stage.at[w], into.at[i])
+        for i, w in enumerate(windows)
+    ]
+    results = [
+        pltpu.make_async_copy(stage.at[w], out.at[w], back.at[i]) for i, w in enumerate(windows)
+    ]
+    for item in arrivals:
+        item.start()
+    for arrival, result in zip(arrivals, results):
+        arrival.wait()
+        result.start()
+    for item in results:
+        item.wait()
 
 
 def on_device(n, rows, cols, front, lower_parts, upper_parts, pattern, row_perm):
@@ -402,9 +402,8 @@
             room(half + piece, width),
             room(half + piece, width),
             room(piece, width),
+            room(piece, width),
             room(n, piece, width),
-            room(piece, width),
-            room(width, width),
             room(width, width, dtype=jnp.bfloat16),
             room(width, width, dtype=jnp.bfloat16),
             room(piece, width),
@@ -418,12 +417,18 @@
     )(
         row_perm, pattern[0].T, front, lower_parts[0], upper_parts[0],
     )
+    anywhere = pl.BlockSpec(memory_space=pl.ANY)
+    count = 4
     return pl.pallas_call(
-        place_kernel,
+        functools.partial(place_kernel, count),
         out_shape=jax.ShapeDtypeStruct((width, width), F32),
-        grid=(4,),
-        in_specs=[pl.BlockSpec((width // 4, width), lambda i: (i, 0))],
-        out_specs=pl.BlockSpec((width // 4, width), lambda i: (i, 0)),
+        in_specs=[anywhere],
+        out_specs=anywhere,
+        scratch_shapes=[
+            room(width, width),
+            pltpu.SemaphoreType.DMA((count,)),
+            pltpu.SemaphoreType.DMA((count,)),
+        ],
     )(factored.reshape(width, width))
 
 

time: 87.9 us -> 84.8 us (0.965)
  Pallas kernels: 87.7 us -> 84.6 us
    pallas_call x1, Pallas kernels: 84.3 us -> 82.6 us  [on_device(): pl.pallas_call(functools.partial(front_kernel, n, rows, cols), out_shape=...]
    pallas_call x1, Pallas kernels: 3.37 us -> 1.98 us  [on_device(): pl.pallas_call(functools.partial(place_kernel, count), out_shape=jax.Shap...]
where the time goes in v7:
time: 84.8 us; the launch traced here: 84.6 us
  Pallas kernels  84.6 us (100%)
    pallas_call x1, Pallas kernels, on_device(): pl.pallas_call(functools.partial(front_kernel, n, rows, cols), out_shape=...  82.6 us
    pallas_call x1, Pallas kernels, on_device(): pl.pallas_call(functools.partial(place_kernel, count), out_shape=jax.Shap...  1.98 us

profile of v7, /device:TPU:168, one launch (start us, length us, event | category | flops | bytes accessed | tf_op | source)
XLA Modules:
  0.0 84.6 jit_solution(12798477486832091597)
XLA Ops:
  0.0 82.6 %shard_map.55 = f32[8,64,512]{2,1,0:T(8,128)} custom-call(s32[1,512]{1,0:T(1,128)} %order.1, s32[2,4]{1,0:T(2,128)} %bitcast.9, f32[512,512]{1,0:T(8,128)} %front.1, f32[512,256]{1,0:T(8,128)} %bitcast.7, f32[256,512]{1,0:T(8,128)} %bitcast.8), custom_call_target="tpu_custom_call" | custom-call | tf_op jit(solution)/shard_map/pallas_call | solution.py:388
  82.6 2.0 %shard_map.56 = f32[512,512]{1,0:T(8,128)} custom-call(f32[512,512]{1,0:T(8,128)} %bitcast.6), custom_call_target="tpu_custom_call" | custom-call | tf_op jit(solution)/shard_map/pallas_call | solution.py:422

commit v8 on v7

--- a/solution.py
+++ b/solution.py
@@ -71,7 +71,7 @@
 
 def front_kernel(n, rows, cols, order, pattern, front, lower, upper, out,
                  onehot, masked, part, base, arrived, own, panel, squares, lows, low_in, inverse,
-                 own_next, second, second_high, second_low, lows_next, low_next_in, inverse_next, own_last, send, recv):
+                 own_next, second, first_high, first_low, second_high, second_low, lows_next, low_next_in, inverse_next, own_last, send, recv):
     me, row, col = lax.axis_index("gz"), lax.axis_index("row"), lax.axis_index("col")
     core = lax.rem(row, 2)
     partner = {"row": row + 1 - 2 * core}
@@ -102,6 +102,24 @@
     picks = onehot[...]
     ordered = [dot(picks, value).astype(jnp.bfloat16) for value in split(masked[...])]
     part[...] = product(ordered, split(upper[...])).reshape(n, piece, width)
+    pl.semaphore_wait(barrier, len(peers))
+    copy = link.batch(n - 1, n - 1)
+    scatter = [
+        copy(part.at[peer], arrived.at[me], k, k, {"gz": peer}) for k, peer in enumerate(across)
+    ]
+
+    def scatter_out():
+        for item in scatter:
+            item.start()
+
+    def reduce():
+        total = base[...]
+        for k, item in enumerate(scatter):
+            item.wait_recv()
+            total = total - arrived[behind[k]]
+        own[...] = total
+
+    pl.when(row != 1)(scatter_out)
     chosen = onehot[pl.ds(pl.multiple_of(me * piece, piece), piece), :]
     high = front[...].astype(jnp.bfloat16)
     rest = front[...] - high.astype(F32)
@@ -109,21 +127,6 @@
     base[...] = (
         dot(chosen, high) + dot(chosen, middle) + dot(chosen, low) - part[me]
     )
-
-    pl.semaphore_wait(barrier, len(peers))
-    copy = link.batch(n - 1, n - 1)
-    scatter = [
-        copy(part.at[peer], arrived.at[me], k, k, {"gz": peer}) for k, peer in enumerate(across)
-    ]
-
-    def reduce():
-        for item in scatter:
-            item.start()
-        total = base[...]
-        for k, item in enumerate(scatter):
-            item.wait_recv()
-            total = total - arrived[behind[k]]
-        own[...] = total
 
     pl.when(row != 1)(reduce)
 
@@ -180,6 +183,7 @@
 
     @pl.when(row == 1)
     def _():
+        scatter_out()
         reduce()
         leave(1)
 
@@ -192,10 +196,15 @@
 
     finish(gather, pair)
 
+    @pl.when(col != 0)
+    def _():
+        first_high[...], first_low[...] = split(panel[0].reshape(width, width))
+
     @pl.when(col == 0)
     def _():
         for step, residual in enumerate(powers(panel[0].reshape(width, width))):
             squares[step] = residual
+        first_high[...], first_low[...] = split(panel[0].reshape(width, width))
 
     land(1)
     own_start = me * piece
@@ -263,7 +272,7 @@
     relay(1)
 
     second[me, mine] = panel[1, me, mine] - product(
-        split(low_in[pl.ds(0, half), :]), split(panel[0].reshape(width, width))
+        split(low_in[pl.ds(0, half), :]), (first_high[...], first_low[...])
     )
     next_gather, next_pair = exchange(second)
     spread(next_gather, next_pair)
@@ -286,7 +295,7 @@
     @pl.when((col != 0) & (row != 0))
     def _():
         own_next[...] = own[...] - product(
-            split(low_in[pl.ds(half, piece), :]), split(panel[0].reshape(width, width))
+            split(low_in[pl.ds(half, piece), :]), (first_high[...], first_low[...])
         )
 
     finish(next_gather, next_pair)
@@ -406,6 +415,8 @@
             room(n, piece, width),
             room(width, width, dtype=jnp.bfloat16),
             room(width, width, dtype=jnp.bfloat16),
+            room(width, width, dtype=jnp.bfloat16),
+            room(width, width, dtype=jnp.bfloat16),
             room(piece, width),
             room(piece, width),
             room(piece, width),

time: 84.8 us -> 84.8 us (level)
  no operation moved by 1% of the time
where the time goes in v8:
time: 84.8 us; the launch traced here: 84.6 us
  Pallas kernels  84.6 us (100%)
    pallas_call x1, Pallas kernels, on_device(): pl.pallas_call(functools.partial(front_kernel, n, rows, cols), out_shape=...  82.6 us
    pallas_call x1, Pallas kernels, on_device(): pl.pallas_call(functools.partial(place_kernel, count), out_shape=jax.Shap...  1.98 us

profile of v8, /device:TPU:168, one launch (start us, length us, event | category | flops | bytes accessed | tf_op | source)
XLA Modules:
  0.0 84.6 jit_solution(9736214347924492411)
XLA Ops:
  0.0 82.6 %shard_map.55 = f32[8,64,512]{2,1,0:T(8,128)} custom-call(s32[1,512]{1,0:T(1,128)} %order.1, s32[2,4]{1,0:T(2,128)} %bitcast.9, f32[512,512]{1,0:T(8,128)} %front.1, f32[512,256]{1,0:T(8,128)} %bitcast.7, f32[256,512]{1,0:T(8,128)} %bitcast.8), custom_call_target="tpu_custom_call" | custom-call | tf_op jit(solution)/shard_map/pallas_call | solution.py:397
  82.6 2.0 %shard_map.56 = f32[512,512]{1,0:T(8,128)} custom-call(f32[512,512]{1,0:T(8,128)} %bitcast.6), custom_call_target="tpu_custom_call" | custom-call | tf_op jit(solution)/shard_map/pallas_call | solution.py:433
